TPU v7x, 128 devices: a whole 4x4x4 slice. The times are simulated.
128 devices in a mesh: row: 4 (over y), col: 4 (over x), depth: 8 (over z, core).
Axes of the slice: x: 4, y: 4, z: 4, core: 2. Of those that a mesh axis runs over, the one named last changes fastest.
Arguments:
- coords: float32 [2, 24576], P(None, ('row', 'col')), may hold values from 0 to 1
- prior: float32 [24576, 16384], P(('row', 'col'), 'depth'), may hold values from -0.057409916 to 0.057409916, as said below
- target: float32 [1024], replicated, may hold values from -6 to 6
- carried: float32 [16384], P('depth'), may hold values from -6 to 6
- variance: float32 [1], replicated, may hold values from 1 to 2
- lengthscale: float32 [1], replicated, may hold values from 0.1 to 0.4
- nugget: float32 [1], replicated, may hold values from 14 to 16
Outputs:
- panels: float32 [24576, 1024], P(('row', 'col'))
- solved: float32 [1024], replicated
Inputs may be any that keep to these rules, and one draw needn't show every extreme that they name: `prior`: independent entries of mean zero.
All inputs are finite; a program needn't handle non-finite values.
Results may differ from a plain program's by a relative error of at most 0.00011.
Values sent between devices are 32-bit elements; how exact they have to be, the bound alone decides.
A program may use at most 128 MiB of HBM per device.

v0:
```python
import jax
import jax.numpy as jnp
from jax import lax
from jax.sharding import PartitionSpec as P

PANEL = 512


root_three = 1.7320508075688772


def spread(block, axis, source):
    block = jnp.where(lax.axis_index(axis) == source, block, jnp.zeros_like(block))
    return lax.psum(block, axis)


def matern(left_xy, right_xy, variance, lengthscale):
    delta_x = left_xy[0][:, None] - right_xy[0][None, :]
    delta_y = left_xy[1][:, None] - right_xy[1][None, :]
    scaled = root_three * jnp.sqrt(delta_x * delta_x + delta_y * delta_y) / lengthscale[0]
    return variance[0] * (1.0 + scaled) * jnp.exp(-scaled)


def inverse_factor(block):
    lower = jnp.linalg.cholesky(block)
    ident = jnp.eye(block.shape[0], dtype=block.dtype)
    return lax.linalg.triangular_solve(lower, ident, left_side=True, lower=True)


def outer_rows(left, right):
    return jnp.einsum("rk,ck->rc", left, right, precision=lax.Precision.HIGHEST)


def panel_block(
    rows_xy,
    row_start,
    summed,
    head_xy,
    inverse_one,
    inverse_two,
    link,
    variance,
    lengthscale,
    nugget,
):
    width = head_xy.shape[1]
    kernel = matern(rows_xy, head_xy, variance, lengthscale)
    row_ids = row_start + jnp.arange(rows_xy.shape[1], dtype=jnp.int32)
    col_ids = jnp.arange(width, dtype=jnp.int32)
    kernel = kernel + jnp.where(row_ids[:, None] == col_ids[None, :], nugget[0], 0.0)
    update = kernel - summed
    first = outer_rows(update[:, :PANEL], inverse_one)
    rest = update[:, PANEL:] - outer_rows(first, link)
    second = outer_rows(rest, inverse_two)
    return jnp.concatenate([first, second], axis=1)


def local(coords, prior, target, carried, variance, lengthscale, nugget):
    highest = lax.Precision.HIGHEST
    width = 2 * PANEL
    rows_dev = prior.shape[0]
    head, head_xy = (
        spread(prior[:width], ("row", "col"), 0),
        spread(coords[:, :width], ("row", "col"), 0),
    )
    gram_first = outer_rows(head, head[:PANEL])
    gram_second = outer_rows(head[PANEL:], head[PANEL:])
    projected = jnp.dot(head, carried, precision=highest)
    gram_first, gram_second, projected = lax.psum((gram_first, gram_second, projected), "depth")
    partial_value = outer_rows(prior, head)
    head_kernel = matern(head_xy, head_xy, variance, lengthscale) + nugget[0] * jnp.eye(
        width, dtype=jnp.float32
    )
    first_head = head_kernel[:, :PANEL] - gram_first
    inverse_one = inverse_factor(first_head[:PANEL])
    link = outer_rows(first_head[PANEL:], inverse_one)
    inverse_two = inverse_factor(head_kernel[PANEL:, PANEL:] - gram_second - outer_rows(link, link))
    residual = target - projected
    z_one = jnp.dot(inverse_one, residual[:PANEL], precision=highest)
    z_two = jnp.dot(
        inverse_two, residual[PANEL:] - jnp.dot(link, z_one, precision=highest), precision=highest
    )
    face = lax.axis_index(("row", "col"))
    summed = lax.psum(partial_value, "depth")
    panels = panel_block(
        coords,
        face * rows_dev,
        summed,
        head_xy,
        inverse_one,
        inverse_two,
        link,
        variance,
        lengthscale,
        nugget,
    )
    return (panels, jnp.concatenate([z_one, z_two]))


def solution(mesh):
    return jax.shard_map(
        local,
        mesh=mesh,
        in_specs=(
            P(None, ("row", "col")),
            P(("row", "col"), "depth"),
            P(),
            P("depth"),
            P(),
            P(),
            P(),
        ),
        out_specs=(P(("row", "col"), None), P()),
        check_vma=False,
    )
```

profile of v0, /device:TPU:13, one launch (start us, length us, event | category | flops | bytes accessed | tf_op | source)
XLA Modules:
  0.0 710.3 jit_solution(17455199424318243919)
XLA Ops:
  7.2 8.2 %slice_select_fusion = f32[1024,2048]{1,0:T(8,128)} fusion(f32[1536,2048]{1,0:T(8,128)} %param.11, pred[]{:T(512)S(6)} %eq.26), kind=kLoop, calls=%fused_computation.4 | loop fusion | flops 2097152 | bytes 16777216 | tf_op jit(solution)/shard_map/jit(_where)/select_n | solution.py:13
  15.5 141.1 %all-reduce.5.cloned.1.call-done = f32[1024,2048]{1,0:T(8,128)} async-done(((f32[1024,2048]{1,0:T(8,128)}), f32[1024,2048]{1,0:T(8,128)}) %all-reduce.5.cloned.1.call-update) | async-done | bytes 8388624 | tf_op jit(solution)/shard_map/psum | solution.py:14
  156.6 10.6 %fusion = f32[512,512]{0,1:T(8,128)} fusion(f32[1024,2048]{1,0:T(8,128)} %all-reduce.5.cloned.1.call-done), kind=kOutput, calls=%fused_computation.9 | convolution fusion | flops 6442450944 | bytes 5242880 | tf_op jit(solution)/shard_map/rk,ck->rc/dot_general | solution.py:31
  167.3 14.9 %fusion.2 = f32[1024,512]{0,1:T(8,128)} fusion(f32[1024,2048]{1,0:T(8,128)S(1)} %copy-done.4), kind=kOutput, calls=%fused_computation.11 | convolution fusion | flops 12884901888 | bytes 14680064 | tf_op jit(solution)/shard_map/rk,ck->rc/dot_general | solution.py:31
  182.2 41.5 %convolution_bitcast_fusion = f32[1536,1024]{0,1:T(8,128)} fusion(f32[1024,2048]{1,0:T(8,128)S(1)} %copy-done.4, f32[1536,2048]{1,0:T(8,128)S(1)} %bitcast.134), kind=kOutput, calls=%fused_computation.8 | convolution fusion | flops 38654705664 | bytes 27262976 | tf_op jit(solution)/shard_map/rk,ck->rc/dot_general | solution.py:31
  225.7 25.5 %psum.42 = f32[2,1024]{1,0:T(2,128)S(1)} all-reduce(f32[2,1024]{1,0:T(2,128)S(1)} %slice_select_fusion.1), channel_id=1, replica_groups=mesh['row'=4,'col'=4,'depth'=8] {'row','col'}, use_global_device_ids=true, to_apply=%region_0.1 | all-reduce | flops 2048 | bytes 16384 | tf_op jit(solution)/shard_map/psum | solution.py:14
  253.1 4.8 select_add_fusion
  257.9 9.5 %fusion.82 = f32[1,1024]{1,0:T(1,128)S(1)} fusion(f32[1024,2048]{1,0:T(8,128)} %all-reduce.5.cloned.1.call-done, f32[2048,1]{0,1:T(1,128)S(1)} %bitcast.132), kind=kOutput, calls=%fused_computation.168 | convolution fusion | flops 25165824 | bytes 8400896 | tf_op jit(solution)/shard_map/dot_general | solution.py:68
  267.4 19.1 %psum.47 = f32[1024]{0:T(1024)S(1)} all-reduce(f32[1024]{0:T(1024)S(1)} %bitcast.139), channel_id=1, replica_groups=mesh['row'=4,'col'=4,'depth'=8] {'depth'}, use_global_device_ids=true, to_apply=%region_13.16 | all-reduce | flops 1024 | bytes 8192 | tf_op jit(solution)/shard_map/psum | solution.py:69
  286.5 52.9 %all-reduce.7.cloned.1.call-done = (f32[1536,1024]{0,1:T(8,128)}, f32[1024,512]{0,1:T(8,128)}, f32[512,512]{0,1:T(8,128)}) async-done(((f32[1536,1024]{0,1:T(8,128)}, f32[1024,512]{0,1:T(8,128)}, f32[512,512]{0,1:T(8,128)}), (f32[1536,1024]{0,1:T(8,128)}, f32[1024,512]{0,1:T(8,128)}, f32[512,512]{0,1:T(8,128)})) %all-reduce.7.cloned.1.call-update) | async-done | bytes 9437200 | tf_op jit(solution)/shard_map/psum | solution.py:84
  339.5 2.6 slice_subtract_fusion
  343.1 2.5 copy.10
  348.2 11.7 %cholesky.286 = f32[128,128]{1,0:T(8,128)S(1)} custom-call(f32[128,128]{1,0:T(8,128)S(1)} %cholesky.426), custom_call_target="Cholesky" | custom-call | tf_op jit(solution)/shard_map/jit(cholesky)/cholesky | solution.py:25
  359.9 9.8 %custom-call.27 = f32[1,128,128]{1,2,0:T(8,128)S(1)} custom-call(f32[1,128,128]{2,1,0:T(8,128)S(1)} %get-tuple-element.66), custom_call_target="InvertDiagBlocksLowerTriangular" | custom-call | tf_op jit(solution)/shard_map/jit(cholesky)/cholesky | solution.py:25
  370.8 1.9 constant_dynamic-update-slice_fusion.5
  374.0 11.7 %cholesky.305 = f32[128,128]{1,0:T(8,128)S(1)} custom-call(f32[128,128]{1,0:T(8,128)S(1)} %cholesky.430), custom_call_target="Cholesky" | custom-call | tf_op jit(solution)/shard_map/jit(cholesky)/cholesky | solution.py:25
  386.4 10.2 %custom-call.28 = f32[1,128,128]{1,2,0:T(8,128)S(1)} custom-call(f32[1,128,128]{2,1,0:T(8,128)S(1)} %get-tuple-element.63), custom_call_target="InvertDiagBlocksLowerTriangular" | custom-call | tf_op jit(solution)/shard_map/jit(cholesky)/cholesky | solution.py:25
  398.9 11.7 %cholesky.326 = f32[128,128]{1,0:T(8,128)S(1)} custom-call(f32[128,128]{1,0:T(8,128)S(1)} %cholesky.435), custom_call_target="Cholesky" | custom-call | tf_op jit(solution)/shard_map/jit(cholesky)/cholesky | solution.py:25
  411.9 9.8 %custom-call.29 = f32[1,128,128]{1,2,0:T(8,128)S(1)} custom-call(f32[1,128,128]{2,1,0:T(8,128)S(1)} %get-tuple-element.60), custom_call_target="InvertDiagBlocksLowerTriangular" | custom-call | tf_op jit(solution)/shard_map/jit(cholesky)/cholesky | solution.py:25
  424.0 11.9 %cholesky.343 = f32[128,128]{1,0:T(8,128)S(1)} custom-call(f32[128,128]{1,0:T(8,128)S(1)} %convolution_subtract_fusion.13), custom_call_target="Cholesky" | custom-call | tf_op jit(solution)/shard_map/jit(cholesky)/cholesky | solution.py:25
  440.2 2.3 select_select_fusion.1
  443.2 11.2 %while.4 = (s32[]{:T(128)}, f32[512,512]{1,0:T(8,128)}, s32[4,2]{0,1:T(2,128)S(1)}, f32[4,128,128]{2,1,0:T(8,128)S(1)}, s32[]{:T(128)}) while((s32[]{:T(128)}, f32[512,512]{1,0:T(8,128)}, s32[4,2]{0,1:T(2,128)S(1)}, f32[4,128,128]{2,1,0:T(8,128)S(1)}, s32[]{:T(128)}) %tuple.58), condition=%wide.while_cond, body=%wide.while_body.sunk | while | flops 2 | bytes 131189 | solution.py:27
  443.8 2.2 bitcast_dynamic-update-slice_fusion.4
  446.6 2.2 bitcast_dynamic-update-slice_fusion.4
  449.4 2.2 bitcast_dynamic-update-slice_fusion.4
  452.2 2.1 bitcast_dynamic-update-slice_fusion.4
  454.4 39.9 %custom-call.30 = f32[4,128,128]{1,2,0:T(8,128)} custom-call(f32[4,128,128]{2,1,0:T(8,128)S(1)} %get-tuple-element.18), custom_call_target="InvertDiagBlocksLowerTriangular" | custom-call | tf_op jit(solution)/shard_map/triangular_solve/custom-call.3 | solution.py:27
  503.8 3.6 fusion.6
  508.4 3.2 convolution_subtract_fusion.1
  514.7 12.1 %cholesky.358 = f32[128,128]{1,0:T(8,128)S(1)} custom-call(f32[128,128]{1,0:T(8,128)S(1)} %cholesky.439), custom_call_target="Cholesky" | custom-call | tf_op jit(solution)/shard_map/jit(cholesky)/cholesky | solution.py:25
  527.5 9.8 %custom-call.31 = f32[1,128,128]{1,2,0:T(8,128)S(1)} custom-call(f32[1,128,128]{2,1,0:T(8,128)S(1)} %get-tuple-element.56), custom_call_target="InvertDiagBlocksLowerTriangular" | custom-call | tf_op jit(solution)/shard_map/jit(cholesky)/cholesky | solution.py:25
  540.6 11.7 %cholesky.377 = f32[128,128]{1,0:T(8,128)S(1)} custom-call(f32[128,128]{1,0:T(8,128)S(1)} %cholesky.443), custom_call_target="Cholesky" | custom-call | tf_op jit(solution)/shard_map/jit(cholesky)/cholesky | solution.py:25
  553.0 9.8 %custom-call.32 = f32[1,128,128]{1,2,0:T(8,128)S(1)} custom-call(f32[1,128,128]{2,1,0:T(8,128)S(1)} %get-tuple-element.53), custom_call_target="InvertDiagBlocksLowerTriangular" | custom-call | tf_op jit(solution)/shard_map/jit(cholesky)/cholesky | solution.py:25
  565.9 13.3 %cholesky.398 = f32[128,128]{1,0:T(8,128)} custom-call(f32[128,128]{1,0:T(8,128)} %cholesky.448), custom_call_target="Cholesky" | custom-call | tf_op jit(solution)/shard_map/jit(cholesky)/cholesky | solution.py:25
  581.4 11.3 %custom-call.33 = f32[1,128,128]{1,2,0:T(8,128)} custom-call(f32[1,128,128]{2,1,0:T(8,128)} %get-tuple-element.50), custom_call_target="InvertDiagBlocksLowerTriangular" | custom-call | tf_op jit(solution)/shard_map/jit(cholesky)/cholesky | solution.py:25
  594.9 11.7 %cholesky.415 = f32[128,128]{1,0:T(8,128)S(1)} custom-call(f32[128,128]{1,0:T(8,128)S(1)} %convolution_subtract_fusion.12), custom_call_target="Cholesky" | custom-call | tf_op jit(solution)/shard_map/jit(cholesky)/cholesky | solution.py:25
  610.9 11.2 %while.5 = (s32[]{:T(128)}, f32[512,512]{1,0:T(8,128)}, s32[4,2]{0,1:T(2,128)S(1)}, f32[4,128,128]{2,1,0:T(8,128)S(1)}, s32[]{:T(128)}) while((s32[]{:T(128)}, f32[512,512]{1,0:T(8,128)}, s32[4,2]{0,1:T(2,128)S(1)}, f32[4,128,128]{2,1,0:T(8,128)S(1)}, s32[]{:T(128)}) %tuple.69), condition=%wide.while_cond.clone, body=%wide.while_body.clone.sunk | while | flops 2 | bytes 131189 | solution.py:27
  611.5 2.2 bitcast_dynamic-update-slice_fusion.5
  614.3 2.2 bitcast_dynamic-update-slice_fusion.5
  617.1 2.2 bitcast_dynamic-update-slice_fusion.5
  620.0 2.1 bitcast_dynamic-update-slice_fusion.5
  622.1 39.3 %custom-call.34 = f32[4,128,128]{1,2,0:T(8,128)S(1)} custom-call(f32[4,128,128]{2,1,0:T(8,128)S(1)} %get-tuple-element.19), custom_call_target="InvertDiagBlocksLowerTriangular" | custom-call | tf_op jit(solution)/shard_map/triangular_solve/custom-call.3 | solution.py:27
  667.3 7.1 %add_subtract_fusion = f32[1536,1024]{0,1:T(8,128)S(1)} fusion(f32[1536,1024]{0,1:T(8,128)} %get-tuple-element.40, f32[]{:T(128)} %bitcast.130, s32[1536]{0:T(1024)S(1)} %copy-done.18, f32[]{:T(128)} %bitcast.128, f32[1024]{0:T(1024)S(1)} %bitcast.138, f32[1536]{0:T(1024)S(1)} %copy-done.17, f32[1024]{0:T(1024)S(1)} %bitcast.136, f32[1536]{0:T(1024)S(1)} %copy-done.16, ...), kind=kLoop, calls=%fused_computation.6 | loop fusion | flops 23592960 | bytes 12609548 | tf_op jit(solution)/shard_map/sub | solution.py:51
  674.5 5.7 fusion.4
  680.2 5.6 convolution_subtract_fusion
  686.8 5.9 fusion.22
  692.8 3.1 pad_maximum_fusion
  695.9 6.6 copy.14
  (147 shorter events, 56.8 us)
Async XLA Ops:
  7.2 250.7 %copy-start = (f32[2048]{0:T(1024)S(1)}, f32[2048]{0:T(1024)}, u32[]{:S(2)}) copy-start(f32[2048]{0:T(1024)} %param.13) | copy-start | bytes 24580
  7.2 149.4 %all-reduce.5.cloned.1.call-start = ((), (), s32[]{:S(2)}) async-start(), calls=%async_computation | async-start | bytes 16777216 | tf_op jit(solution)/shard_map/psum | solution.py:14
  15.5 324.0 %all-reduce.7.cloned.1.call-start = ((), (), s32[]{:S(2)}) async-start(), calls=%async_computation.1 | async-start | bytes 18874368 | tf_op jit(solution)/shard_map/psum | solution.py:84
  156.6 10.7 %copy-start.4 = (f32[1024,2048]{1,0:T(8,128)S(1)}, f32[1024,2048]{1,0:T(8,128)}, u32[]{:S(2)}) copy-start(f32[1024,2048]{1,0:T(8,128)} %all-reduce.5.cloned.1.call-done) | copy-start | bytes 25165828
  156.6 25.5 %slice-start = ((s8[12582912]{0:T(1024)(128)(4,1)}), s8[4194304]{0:T(1024)(128)(4,1)S(1)}, s32[]{:S(2)}) async-start(s8[12582912]{0:T(1024)(128)(4,1)} %bitcast.133), calls=%async_computation.2 | async-start | bytes 8388608
  167.3 14.9 %slice-start.1 = ((s8[12582912]{0:T(1024)(128)(4,1)}), s8[4194304]{0:T(1024)(128)(4,1)S(1)}, s32[]{:S(2)}) async-start(s8[12582912]{0:T(1024)(128)(4,1)} %bitcast.133), calls=%async_computation.3 | async-start | bytes 8388608
  167.3 14.9 %slice-start.2 = ((s8[12582912]{0:T(1024)(128)(4,1)}), s8[4194304]{0:T(1024)(128)(4,1)S(1)}, s32[]{:S(2)}) async-start(s8[12582912]{0:T(1024)(128)(4,1)} %bitcast.133), calls=%async_computation.4 | async-start | bytes 8388608
  223.7 2.0 copy-start.15
  253.1 247.7 %copy-start.2 = (f32[512,512]{1,0:T(8,128)}, f32[512,512]{1,0:T(8,128)S(1)}, u32[]{:S(2)}) copy-start(f32[512,512]{1,0:T(8,128)S(1)} %fusion.10) | copy-start | bytes 3145732
  257.9 28.6 %copy-start.23 = (f32[1024]{0:T(1024)S(1)}, f32[1024]{0:T(1024)}, u32[]{:S(2)}) copy-start(f32[1024]{0:T(1024)} %param.12) | copy-start | bytes 12292
  286.5 56.6 %copy-start.19 = (f32[1024]{0:T(1024)}, f32[1024]{0:T(1024)S(1)}, u32[]{:S(2)}) copy-start(f32[1024]{0:T(1024)S(1)} %sub.102) | copy-start | bytes 12292
  347.2 1.0 copy-start.10
  495.6 11.8 %slice-start.3 = ((f32[1024]{0:T(1024)}), f32[512]{0:T(512)S(1)}, s32[]{:S(2)}) async-start(f32[1024]{0:T(1024)} %copy-done.19), calls=%async_computation.5 | async-start | bytes 4096 | tf_op jit(solution)/shard_map/slice | solution.py:79
  498.1 10.3 %copy-start.5 = (f32[128,512]{1,0:T(8,128)}, f32[128,512]{1,0:T(8,128)S(1)}, u32[]{:S(2)}) copy-start(f32[128,512]{1,0:T(8,128)S(1)} %fusion.59) | copy-start | bytes 786436
  498.1 10.3 %copy-start.13 = (f32[512,512]{0,1:T(8,128)S(1)}, f32[512,512]{0,1:T(8,128)}, u32[]{:S(2)}) copy-start(f32[512,512]{0,1:T(8,128)} %get-tuple-element.42) | copy-start | bytes 3145732
  500.8 10.7 %copy-start.7 = (f32[128,512]{1,0:T(8,128)}, f32[128,512]{1,0:T(8,128)S(1)}, u32[]{:S(2)}) copy-start(f32[128,512]{1,0:T(8,128)S(1)} %fusion.57) | copy-start | bytes 786436
  503.8 7.8 %copy-start.11 = (f32[128,512]{1,0:T(8,128)}, f32[128,512]{1,0:T(8,128)S(1)}, u32[]{:S(2)}) copy-start(f32[128,512]{1,0:T(8,128)S(1)} %fusion.56) | copy-start | bytes 786436
  507.3 5.2 copy-start.20
  508.4 4.2 copy-start.21
  513.7 1.0 copy-start.9
  514.7 146.7 %copy-start.3 = (f32[512,512]{1,0:T(8,128)S(1)}, f32[512,512]{1,0:T(8,128)}, u32[]{:S(2)}) copy-start(f32[512,512]{1,0:T(8,128)} %copy-done.2) | copy-start | bytes 3145732
  539.9 0.7 copy-start.14
  609.7 57.6 %copy-start.16 = (f32[1536]{0:T(1024)S(1)}, f32[1536]{0:T(1024)}, u32[]{:S(2)}) copy-start(f32[1536]{0:T(1024)} %get-tuple-element.22) | copy-start | bytes 18436
  609.7 57.6 %copy-start.17 = (f32[1536]{0:T(1024)S(1)}, f32[1536]{0:T(1024)}, u32[]{:S(2)}) copy-start(f32[1536]{0:T(1024)} %get-tuple-element.23) | copy-start | bytes 18436
  609.7 57.6 %copy-start.18 = (s32[1536]{0:T(1024)S(1)}, s32[1536]{0:T(1024)}, u32[]{:S(2)}) copy-start(s32[1536]{0:T(1024)} %iota_add_fusion) | copy-start | bytes 18436
  667.3 7.2 %copy-start.6 = (f32[128,512]{1,0:T(8,128)S(1)}, f32[128,512]{1,0:T(8,128)}, u32[]{:S(2)}) copy-start(f32[128,512]{1,0:T(8,128)} %copy-done.5) | copy-start | bytes 786436
  667.3 7.2 %copy-start.8 = (f32[128,512]{1,0:T(8,128)S(1)}, f32[128,512]{1,0:T(8,128)}, u32[]{:S(2)}) copy-start(f32[128,512]{1,0:T(8,128)} %copy-done.7) | copy-start | bytes 786436
  667.3 7.2 %copy-start.12 = (f32[128,512]{1,0:T(8,128)S(1)}, f32[128,512]{1,0:T(8,128)}, u32[]{:S(2)}) copy-start(f32[128,512]{1,0:T(8,128)} %copy-done.11) | copy-start | bytes 786436
  680.2 5.6 copy-start.24
  692.7 10.3 %copy-start.1 = (f32[2048]{0:T(1024)S(1)}, f32[2048]{0:T(1024)}, u32[]{:S(2)}) copy-start(f32[2048]{0:T(1024)} %param.13) | copy-start | bytes 24580
  695.9 6.6 copy-start.22
Sparse Core Ops, SparseCore 0:
  15.6 140.9 all-reduce.4
  223.9 115.5 all-reduce.6
where the time goes:
time: 717 us; the launch traced here: 710 us
  other arithmetic  277 us (39%)
  waiting for transfers between devices  194 us (27%)
  matrix products  134 us (19%)
  blocking collectives  44.6 us (6%)
  local copies, waits for them, and re-layouts  38.7 us (5%)
  between operations  22 us (3%)
    another operation x29, other arithmetic, inverse_factor(): lower = jnp.linalg.cholesky(block)  165 us
    psum x1, waiting for transfers between devices, spread(): return lax.psum(block, axis)  141 us
    dot_general x8, matrix products, outer_rows(): return jnp.einsum('rk,ck->rc', left, right, precision=lax.Precision.HIGHEST)  91 us
    another operation x5, other arithmetic, inverse_factor(): return lax.linalg.triangular_solve(lower, ident, left_side=True, lower=True)  83.3 us
    psum x1, waiting for transfers between devices, local(): summed = lax.psum(partial_value, 'depth')  52.9 us
    psum x1, blocking collectives, spread(): return lax.psum(block, axis)  25.5 us
    another operation x27, local copies, waits for them, and re-layouts, inverse_factor(): return lax.linalg.triangular_solve(lower, ident, left_side=True, lower=True)  22.9 us
    psum x1, blocking collectives, local(): lax.psum((gram_first, gram_second, projected), 'depth')  19.1 us
  transfers between devices with their start and end apart: 2, of which 2 were waited for; matrix products, arithmetic and copies ran while one was open for 2% of the time, Pallas kernels for 0%

commit v1 on v0

v1 whole, which is shorter than its diff:
```python
import functools

import jax
import jax.numpy as jnp
from jax import lax
from jax.experimental import pallas as pl
from jax.experimental.pallas import tpu as pltpu
from jax.sharding import PartitionSpec as P

f32 = jnp.float32
MESH = pl.DeviceIdType.MESH
B = 128
root_three = 1.7320508075688772


def split(x):
    hi = x.astype(jnp.bfloat16)
    return hi, (x - hi.astype(f32)).astype(jnp.bfloat16)


def iota8():
    shape = (8, B)
    return lax.broadcasted_iota(jnp.int32, shape, 0), lax.broadcasted_iota(jnp.int32, shape, 1)

def base(x, b=32):
    n=B; row8,col8=iota8()
    T=n//8; nt=b//8
    X=[x[8*t:8*t+8] for t in range(T)]
    out=[]
    for blk in range(n//b):
        c0=blk*b; t0=c0//8
        C=[[jnp.broadcast_to(X[t0+t][:,c0+k:c0+k+1],(8,n)) for k in range(8*t+8)] for t in range(nt)]
        inb=(col8>=c0)&(col8<c0+b)
        E=[jnp.where(inb,(col8==row8+(c0+8*t)).astype(f32),X[t0+t]) for t in range(nt)]
        scale=[None]*nt
        for j in range(b):
            tj,sj=divmod(j,8)
            p=C[tj][j][sj:sj+1,:]
            pinv=1.0/p
            rs=lax.rsqrt(p)
            scale[tj]=jnp.broadcast_to(rs,(8,n)) if sj==0 else jnp.where(row8==sj,rs,scale[tj])
            er=E[tj][sj:sj+1,:]*pinv
            rk={}
            for k in range(j+1,b):
                tk,sk=divmod(k,8)
                rk[k]=C[tk][j][sk:sk+1,:]*pinv
            for t in range(tj,nt):
                c=C[t][j]
                for k in range(j+1,8*t+8):
                    C[t][k]=C[t][k]-c*rk[k]
                ce=jnp.where(row8>sj,c,0.0) if t==tj else c
                if not (t==tj and sj==7):
                    E[t]=E[t]-ce*er
        U=[E[t]*scale[t] for t in range(nt)]
        out+=U
        if c0+b<n:
            u=jnp.concatenate(U,axis=0)
            at=u.T[c0+b:]
            ah,al=split(at); bh,bl=split(u)
            l=jnp.concatenate([ah,al,ah],axis=1); r=jnp.concatenate([bh,bh,bl],axis=0)
            d=jnp.dot(l,r,preferred_element_type=f32)
            for t in range(t0+nt,T):
                o=8*t-(c0+b)
                X[t]=jnp.where(inb,0.0,X[t])-d[o:o+8]
    w=jnp.concatenate(out,axis=0)
    rr=lax.broadcasted_iota(jnp.int32,(n,n),0); cc=lax.broadcasted_iota(jnp.int32,(n,n),1)
    return jnp.where(cc<=rr,w,0.0)


WAY_IN = {(0, 1): 0, (3, 0): 2, (0, 3): 0, (1, 0): 2, (0, 2): 0, (2, 0): 2, (1, 1): 2, (3, 1): 1, (3, 3): 3,
          (1, 3): 2, (1, 2): 2, (2, 1): 1, (3, 2): 3, (2, 3): 2, (2, 2): 1}
STEP = ((1, 0), (0, 1), (-1, 0), (0, -1))

def tree_kids():
    kids = [[[] for _ in range(4)] for _ in range(4)]
    for node, way in WAY_IN.items():
        for q in range(4):
            x, y = node
            for _ in range(q):
                x, y = (-y) % 4, x
            e = (way + q) % 4
            kids[q][e].append((x - STEP[e][0]) % 4 + 4 * ((y - STEP[e][1]) % 4))
    return kids
KIDS = tree_kids()

def tree_depths():
    out = [[0] * 16 for _ in range(4)]
    for node in WAY_IN:
        u, k = node, 0
        while u != (0, 0):
            s = STEP[WAY_IN[u]]
            u, k = ((u[0] - s[0]) % 4, (u[1] - s[1]) % 4), k + 1
        x, y = node
        for q in range(4):
            out[q][x + 4 * y] = k
            x, y = (-y) % 4, x
    return out
DEPTH = tree_depths()


def bkernel(R, D, prior_ref, out_ref, head, send_sem, recv_sem, osem):
    x, y = lax.axis_index("col"), lax.axis_index("row")
    z = lax.axis_index("depth")
    node = x + 4 * y
    nbr = [{"col": lax.rem(x + 4 + sx, 4), "row": lax.rem(y + 4 + sy, 4)} for sx, sy in STEP]
    sends = {}
    for q in range(4):
        for e in range(4):
            ks = KIDS[q][e]
            if ks:
                sends[q, e] = functools.reduce(jnp.logical_or, [node == k for k in ks])
    barrier = pltpu.get_barrier_semaphore()
    for e in range(4):
        pl.semaphore_signal(barrier, inc=1, device_id=nbr[e], device_id_type=MESH)
    pl.semaphore_wait(barrier, 4)
    C = 256 // R
    def rows(q, c):
        return pl.ds(pl.multiple_of((c * 4 + q) * R, R), R)
    def copy(q, e, c, src):
        return pltpu.make_async_remote_copy(src_ref=src.at[rows(q, c)], dst_ref=head.at[rows(q, c)],
            send_sem=send_sem.at[q, e], recv_sem=recv_sem.at[q, c], device_id=nbr[e], device_id_type=MESH)
    @pl.when(node == 0)
    def _():
        def body(c, _):
            for q in range(4):
                for e in range(4):
                    if (q, e) in sends and 0 in KIDS[q][e]:
                        copy(q, e, c, prior_ref).start()
            return 0
        lax.fori_loop(0, C, body, 0)
        cp = pltpu.make_async_copy(prior_ref.at[pl.ds(0, 1024)], head, osem)
        cp.start(); cp.wait()
    depth = [sum(jnp.where(node == v, D * DEPTH[q][v], 0) for v in range(1, 16)) for q in range(4)]
    deepest = max(max(d) for d in DEPTH)
    @pl.when(node != 0)
    def _():
        def body(s, _):
            for q in range(4):
                c = s + D - depth[q]
                @pl.when((c >= 0) & (c < C))
                def _():
                    copy(q, 0, c, head).wait_recv()
                    for e in range(4):
                        if (q, e) in sends and any(k != 0 for k in KIDS[q][e]):
                            @pl.when(sends[q, e])
                            def _():
                                copy(q, e, c, head).start()
            return 0
        lax.fori_loop(0, C + D * (deepest - 1), body, 0)
    for (q, e), has in sends.items():
        @pl.when(has)
        def _():
            pltpu.make_async_remote_copy(src_ref=head.at[pl.ds(0, 256)], dst_ref=head.at[pl.ds(0, 256)],
                send_sem=send_sem.at[q, e], recv_sem=recv_sem.at[0, 0], device_id=nbr[e], device_id_type=MESH).wait_send()
    cp = pltpu.make_async_copy(head, out_ref, osem)
    cp.start(); cp.wait()

def bcast(prior, R=16, D=1):
    return pl.pallas_call(
        functools.partial(bkernel, R, D),
        out_shape=jax.ShapeDtypeStruct((1024, 2048), f32),
        in_specs=[pl.BlockSpec(memory_space=pl.ANY)],
        out_specs=pl.BlockSpec(memory_space=pl.ANY),
        scratch_shapes=[pltpu.VMEM((1024, 2048), f32), pltpu.SemaphoreType.DMA((4, 4)), pltpu.SemaphoreType.DMA((4, 256 // R)), pltpu.SemaphoreType.DMA],
        compiler_params=pltpu.CompilerParams(collective_id=1, has_side_effects=True, vmem_limit_bytes=50 << 20),
    )(prior)


def sl(a):
    h, l = split(a); return jnp.concatenate([h, l, h], axis=1)
def sr(b):
    h, l = split(b); return jnp.concatenate([h, h, l], axis=0)
def mm(l, r):
    return jnp.dot(l, r, preferred_element_type=f32)

def chol_kernel(a_ref, w_ref, b_ref, m_ref):
    n = a_ref.shape[0]
    nb = n // B
    b_ref[...] = a_ref[...]
    ri = lax.broadcasted_iota(jnp.int32, (B, n), 0)
    ci = lax.broadcasted_iota(jnp.int32, (B, n), 1)
    m_ref[...] = base(b_ref[0:B, 0:B])
    def step(k, _):
        ks = pl.multiple_of(k * B, B)
        kn = pl.multiple_of(jnp.minimum(k + 1, nb - 1) * B, B)
        m = m_ref[...]
        inblk = (ci >= ks) & (ci < ks + B)
        row = jnp.where(inblk, (ci == ri + ks).astype(f32), b_ref[pl.ds(ks, B), :])
        r = mm(sl(m), sr(row))
        w_ref[pl.ds(ks, B), :] = jnp.where(ci < ks + B, r, 0.0)
        rs = sr(r)
        mt = sr(m.T)
        g = mm(sl(b_ref[pl.ds(kn, B), pl.ds(ks, B)]), mt)
        nxt = jnp.where(inblk, 0.0, b_ref[pl.ds(kn, B), :]) - mm(sl(g), rs)
        b_ref[pl.ds(kn, B), :] = nxt
        m_ref[...] = base(b_ref[pl.ds(kn, B), pl.ds(kn, B)])
        rows = lax.broadcasted_iota(jnp.int32, (n, 1), 0)
        act = rows >= ks + 2 * B
        g = jnp.where(act, mm(sl(b_ref[:, pl.ds(ks, B)]), mt), 0.0)
        gs = sl(g)
        for i in range(2, nb):
            z = (act[i * B:(i + 1) * B]) & inblk
            cur = jnp.where(z, 0.0, b_ref[i * B:(i + 1) * B, :])
            b_ref[i * B:(i + 1) * B, :] = cur - mm(gs[i * B:(i + 1) * B], rs)
        return 0
    lax.fori_loop(0, nb, step, 0)

def chol_inv(a):
    n = a.shape[0]
    return pl.pallas_call(
        chol_kernel,
        out_shape=jax.ShapeDtypeStruct((n, n), jnp.float32),
        in_specs=[pl.BlockSpec(memory_space=pltpu.VMEM)],
        out_specs=pl.BlockSpec(memory_space=pltpu.VMEM),
        scratch_shapes=[pltpu.VMEM((n, n), jnp.float32), pltpu.VMEM((B, B), jnp.float32)],
        compiler_params=pltpu.CompilerParams(vmem_limit_bytes=40 << 20),
    )(a)


def matern(left_xy, right_xy, variance, lengthscale):
    delta_x = left_xy[0][:, None] - right_xy[0][None, :]
    delta_y = left_xy[1][:, None] - right_xy[1][None, :]
    scaled = root_three * jnp.sqrt(delta_x * delta_x + delta_y * delta_y) / lengthscale[0]
    return variance[0] * (1.0 + scaled) * jnp.exp(-scaled)


def outer_rows(left, right):
    return jnp.einsum("rk,ck->rc", left, right, precision=lax.Precision.HIGH)


def local(coords, prior, target, carried, variance, lengthscale, nugget):
    highest = lax.Precision.HIGHEST
    width = 1024
    rows_dev = prior.shape[0]
    face = lax.axis_index(("row", "col"))
    head = bcast(prior, 8, 3)
    xy = jnp.where(face == 0, coords[:, :width], 0.0)
    head_xy = lax.psum(xy, ("row", "col"))
    gram = outer_rows(head, head)
    projected = jnp.dot(head, carried, precision=highest)
    gram, projected, summed = lax.psum((gram, projected, outer_rows(prior, head)), "depth")
    head_kernel = matern(head_xy, head_xy, variance, lengthscale) + nugget[0] * jnp.eye(width, dtype=f32)
    inverse = chol_inv(head_kernel - gram)
    solved = jnp.dot(inverse, target - projected, precision=highest)
    kernel = matern(coords, head_xy, variance, lengthscale)
    row_ids = face * rows_dev + jnp.arange(rows_dev, dtype=jnp.int32)
    col_ids = jnp.arange(width, dtype=jnp.int32)
    kernel = kernel + jnp.where(row_ids[:, None] == col_ids[None, :], nugget[0], 0.0)
    panels = outer_rows(kernel - summed, inverse)
    return (panels, solved)


def solution(mesh):
    return jax.shard_map(
        local,
        mesh=mesh,
        in_specs=(
            P(None, ("row", "col")),
            P(("row", "col"), "depth"),
            P(),
            P("depth"),
            P(),
            P(),
            P(),
        ),
        out_specs=(P(("row", "col"), None), P()),
        check_vma=False,
    )
```

time: 717 us -> 326 us (0.45)
  the two profiles are of different devices: /device:TPU:13 before, /device:TPU:1 now
where the time goes in v1:
time: 326 us; the launch traced here: 321 us
  Pallas kernels  94.8 us (29%)
  matrix products  73.2 us (22%)
  waiting for transfers between devices  70.4 us (22%)
  blocking collectives  60.1 us (18%)
  between operations  16.4 us (5%)
  other arithmetic  5.48 us (2%)
    psum x1, waiting for transfers between devices, local(): lax.psum((gram, projected, outer_rows(prior, head)), 'depth')  70.4 us
    dot_general x3, matrix products, outer_rows(): return jnp.einsum('rk,ck->rc', left, right, precision=lax.Precision.HIGH)  59.5 us
    pallas_call x1, Pallas kernels, bcast(): pl.pallas_call(functools.partial(bkernel, R, D), out_shape=jax.ShapeDtype...  52.8 us
    psum x1, blocking collectives, local(): head_xy = lax.psum(xy, ('row', 'col'))  45.6 us
    pallas_call x1, Pallas kernels, chol_inv(): pl.pallas_call(chol_kernel, out_shape=jax.ShapeDtypeStruct((n, n), jnp.fl...  42 us
    psum x1, blocking collectives, local(): lax.psum((gram, projected, outer_rows(prior, head)), 'depth')  14.5 us
    dot_general x1, matrix products, local(): projected = jnp.dot(head, carried, precision=highest)  9.4 us
  transfers between devices with their start and end apart: 1, of which 1 were waited for; matrix products, arithmetic and copies ran while one was open for 3% of the time, Pallas kernels for 0%

profile of v1, /device:TPU:1, one launch (start us, length us, event | category | flops | bytes accessed | tf_op | source)
XLA Modules:
  0.0 320.5 jit_solution(6702611206513395276)
XLA Ops:
  7.2 0.0 copy-start
  7.2 0.0 all-reduce.3.cloned.1.call-start
  7.2 0.0 slice-start
  7.2 0.0 slice-start.1
  7.2 52.8 %shard_map.86 = f32[1024,2048]{1,0:T(8,128)} custom-call(f32[1536,2048]{1,0:T(8,128)} %prior_ref.1), custom_call_target="tpu_custom_call" | custom-call | tf_op jit(solution)/shard_map/pallas_call | solution.py:159
  60.1 0.0 copy-start.1
  60.1 0.0 slice-start.2
  60.1 20.4 %fusion.33 = f32[1024,1024]{1,0:T(8,128)} fusion(f32[1024,2048]{1,0:T(8,128)} %shard_map.86), kind=kOutput, calls=%fused_computation.40 | convolution fusion | flops 12884901888 | bytes 12582912 | tf_op jit(solution)/shard_map/rk,ck->rc/dot_general | solution.py:228
  80.5 0.0 slice-done
  80.5 0.0 slice-done.1
  80.5 0.0 copy-done.1
  80.5 0.0 slice-done.2
  80.5 22.8 %fusion.32 = f32[1536,1024]{1,0:T(8,128)} fusion(f32[1536,2048]{1,0:T(8,128)S(1)} %bitcast.26, f32[1024,2048]{1,0:T(8,128)S(1)} %copy-done.1), kind=kOutput, calls=%fused_computation.39 | convolution fusion | flops 19327352832 | bytes 27262976 | tf_op jit(solution)/shard_map/rk,ck->rc/dot_general | solution.py:228
  103.3 0.0 all-reduce.3.cloned.1.call-update
  103.3 0.0 copy-start.3
  103.3 0.0 copy-start.2
  105.3 0.0 copy-done
  105.3 9.4 %fusion.34 = f32[1,1024]{1,0:T(1,128)S(1)} fusion(f32[1024,2048]{1,0:T(8,128)} %shard_map.86, f32[2048,1]{0,1:T(1,128)S(1)} %bitcast.24), kind=kOutput, calls=%fused_computation.41 | convolution fusion | flops 25165824 | bytes 8400896 | tf_op jit(solution)/shard_map/dot_general | solution.py:240
  114.7 14.5 %psum.31 = f32[1024]{0:T(1024)S(1)} all-reduce(f32[1024]{0:T(1024)S(1)} %bitcast.31), channel_id=1, replica_groups=mesh['row'=4,'col'=4,'depth'=8] {'depth'}, use_global_device_ids=true, to_apply=%region_3.4 | all-reduce | flops 1024 | bytes 8192 | tf_op jit(solution)/shard_map/psum | solution.py:241
  129.2 0.0 copy-done.3
  129.3 0.0 copy-done.2
  129.3 45.6 %psum.28 = f32[2,1024]{1,0:T(2,128)S(1)} all-reduce(f32[2,1024]{1,0:T(2,128)S(1)} %slice_select_fusion), channel_id=1, replica_groups=mesh['row'=4,'col'=4,'depth'=8] {'row','col'}, use_global_device_ids=true, to_apply=%region_0.1 | all-reduce | flops 2048 | bytes 16384 | tf_op jit(solution)/shard_map/psum | solution.py:238
  174.9 70.4 %all-reduce.3.cloned.1.call-done = (f32[1024,1024]{1,0:T(8,128)}, f32[1536,1024]{1,0:T(8,128)}) async-done(((f32[1024,1024]{1,0:T(8,128)}, f32[1536,1024]{1,0:T(8,128)}), (f32[1024,1024]{1,0:T(8,128)}, f32[1536,1024]{1,0:T(8,128)})) %all-reduce.3.cloned.1.call-update) | async-done | bytes 10485776 | tf_op jit(solution)/shard_map/psum | solution.py:241
  245.3 0.0 slice-start.3
  245.3 5.5 %add_subtract_fusion.a_ref = f32[1024,1024]{1,0:T(8,128)S(1)} fusion(f32[1024,1024]{1,0:T(8,128)} %get-tuple-element.4, f32[]{:T(128)} %bitcast.23, f32[]{:T(128)} %bitcast.21, f32[1024]{0:T(1024)S(1)} %bitcast.29, f32[1024]{0:T(1024)S(1)} %bitcast.27, f32[]{:T(128)} %bitcast.19), kind=kLoop, calls=%fused_computation.18 | loop fusion | flops 15728640 | bytes 8396812 | tf_op jit(solution)/shard_map/sub | solution.py:243
  250.8 0.0 slice-start.4
  250.8 42.0 %shard_map.87 = f32[1024,1024]{1,0:T(8,128)S(1)} custom-call(f32[1024,1024]{1,0:T(8,128)S(1)} %add_subtract_fusion.a_ref), custom_call_target="tpu_custom_call" | custom-call | tf_op jit(solution)/shard_map/pallas_call | solution.py:210
  292.8 4.2 %fusion.35 = f32[1,1024]{1,0:T(1,128)} fusion(f32[1024,1024]{1,0:T(8,128)S(1)} %shard_map.87, f32[1024,1]{0,1:T(1,128)S(1)} %bitcast.32), kind=kOutput, calls=%fused_computation.42 | convolution fusion | flops 12582912 | bytes 4202496 | tf_op jit(solution)/shard_map/dot_general | solution.py:244
  297.0 0.0 slice-done.3
  297.0 0.0 slice-done.4
  297.0 16.4 %fusion = f32[1536,1024]{1,0:T(8,128)} fusion(f32[1024,1024]{1,0:T(8,128)S(1)} %shard_map.87, f32[1536,1024]{1,0:T(8,128)S(1)} %bitcast.35, f32[]{:T(128)} %bitcast.22, s32[1536]{0:T(1024)S(1)} %iota_add_fusion, f32[]{:T(128)} %bitcast.20, f32[1024]{0:T(1024)S(1)} %bitcast.30, f32[1536]{0:T(1024)S(1)} %get-tuple-element.3, f32[1024]{0:T(1024)S(1)} %bitcast.28, ...), kind=kOutput, calls=%fused_computation | convolution fusion | flops 9687269376 | bytes 16803852 | tf_op jit(solution)/shard_map/rk,ck->rc/dot_general | solution.py:228
  (7 shorter events, 0.1 us)
Async XLA Ops:
  7.2 98.1 %copy-start = (f32[2048]{0:T(1024)S(1)}, f32[2048]{0:T(1024)}, u32[]{:S(2)}) copy-start(f32[2048]{0:T(1024)} %param.10) | copy-start | bytes 24580
  7.2 238.1 %all-reduce.3.cloned.1.call-start = ((), (), s32[]{:S(2)}) async-start(), calls=%async_computation | async-start | bytes 20971520 | tf_op jit(solution)/shard_map/psum | solution.py:241
  7.2 73.3 %slice-start = ((s8[12582912]{0:T(1024)(128)(4,1)}), s8[4194304]{0:T(1024)(128)(4,1)S(1)}, s32[]{:S(2)}) async-start(s8[12582912]{0:T(1024)(128)(4,1)} %bitcast.25), calls=%async_computation.1 | async-start | bytes 8388608
  7.2 73.3 %slice-start.1 = ((s8[12582912]{0:T(1024)(128)(4,1)}), s8[4194304]{0:T(1024)(128)(4,1)S(1)}, s32[]{:S(2)}) async-start(s8[12582912]{0:T(1024)(128)(4,1)} %bitcast.25), calls=%async_computation.2 | async-start | bytes 8388608
  60.1 20.4 %copy-start.1 = (f32[1024,2048]{1,0:T(8,128)S(1)}, f32[1024,2048]{1,0:T(8,128)}, u32[]{:S(2)}) copy-start(f32[1024,2048]{1,0:T(8,128)} %shard_map.86) | copy-start | bytes 25165828
  60.1 20.4 %slice-start.2 = ((s8[12582912]{0:T(1024)(128)(4,1)}), s8[4194304]{0:T(1024)(128)(4,1)S(1)}, s32[]{:S(2)}) async-start(s8[12582912]{0:T(1024)(128)(4,1)} %bitcast.25), calls=%async_computation.3 | async-start | bytes 8388608
  103.3 25.9 %copy-start.3 = (f32[1024]{0:T(1024)S(1)}, f32[1024]{0:T(1024)}, u32[]{:S(2)}) copy-start(f32[1024]{0:T(1024)} %param.9) | copy-start | bytes 12292
  103.3 25.9 %copy-start.2 = (f32[2,1536]{1,0:T(2,128)S(1)}, f32[2,1536]{1,0:T(2,128)}, u32[]{:S(2)}) copy-start(f32[2,1536]{1,0:T(2,128)} %param.7) | copy-start | bytes 36868
  245.3 51.7 %slice-start.3 = ((s8[6291456]{0:T(1024)(128)(4,1)}), s8[4194304]{0:T(1024)(128)(4,1)S(1)}, s32[]{:S(2)}) async-start(s8[6291456]{0:T(1024)(128)(4,1)} %bitcast.34), calls=%async_computation.4 | async-start | bytes 8388608
  250.8 46.3 %slice-start.4 = ((s8[6291456]{0:T(1024)(128)(4,1)}), s8[2097152]{0:T(1024)(128)(4,1)S(1)}, s32[]{:S(2)}) async-start(s8[6291456]{0:T(1024)(128)(4,1)} %bitcast.34), calls=%async_computation.5 | async-start | bytes 4194304
Sparse Core Ops, SparseCore 0:
  103.4 141.8 all-reduce.2

commit v2 on v1

v2 whole, which is shorter than its diff:
```python
import functools

import jax
import jax.numpy as jnp
from jax import lax
from jax.experimental import pallas as pl
from jax.experimental.pallas import tpu as pltpu
from jax.sharding import PartitionSpec as P

f32 = jnp.float32
MESH = pl.DeviceIdType.MESH
B = 128
root_three = 1.7320508075688772


def split(x):
    hi = x.astype(jnp.bfloat16)
    return hi, (x - hi.astype(f32)).astype(jnp.bfloat16)


def iota8():
    shape = (8, B)
    return lax.broadcasted_iota(jnp.int32, shape, 0), lax.broadcasted_iota(jnp.int32, shape, 1)

def base(x, b=32):
    n=B; row8,col8=iota8()
    T=n//8; nt=b//8
    X=[x[8*t:8*t+8] for t in range(T)]
    out=[]
    for blk in range(n//b):
        c0=blk*b; t0=c0//8
        C=[[jnp.broadcast_to(X[t0+t][:,c0+k:c0+k+1],(8,n)) for k in range(8*t+8)] for t in range(nt)]
        inb=(col8>=c0)&(col8<c0+b)
        E=[jnp.where(inb,(col8==row8+(c0+8*t)).astype(f32),X[t0+t]) for t in range(nt)]
        scale=[None]*nt
        for j in range(b):
            tj,sj=divmod(j,8)
            p=C[tj][j][sj:sj+1,:]
            pinv=1.0/p
            rs=lax.rsqrt(p)
            scale[tj]=jnp.broadcast_to(rs,(8,n)) if sj==0 else jnp.where(row8==sj,rs,scale[tj])
            er=E[tj][sj:sj+1,:]*pinv
            rk={}
            for k in range(j+1,b):
                tk,sk=divmod(k,8)
                rk[k]=C[tk][j][sk:sk+1,:]*pinv
            for t in range(tj,nt):
                c=C[t][j]
                for k in range(j+1,8*t+8):
                    C[t][k]=C[t][k]-c*rk[k]
                ce=jnp.where(row8>sj,c,0.0) if t==tj else c
                if not (t==tj and sj==7):
                    E[t]=E[t]-ce*er
        U=[E[t]*scale[t] for t in range(nt)]
        out+=U
        if c0+b<n:
            u=jnp.concatenate(U,axis=0)
            at=u.T[c0+b:]
            ah,al=split(at); bh,bl=split(u)
            l=jnp.concatenate([ah,al,ah],axis=1); r=jnp.concatenate([bh,bh,bl],axis=0)
            d=jnp.dot(l,r,preferred_element_type=f32)
            for t in range(t0+nt,T):
                o=8*t-(c0+b)
                X[t]=jnp.where(inb,0.0,X[t])-d[o:o+8]
    w=jnp.concatenate(out,axis=0)
    rr=lax.broadcasted_iota(jnp.int32,(n,n),0); cc=lax.broadcasted_iota(jnp.int32,(n,n),1)
    return jnp.where(cc<=rr,w,0.0)


WAY_IN = {(0, 1): 0, (3, 0): 2, (0, 3): 0, (1, 0): 2, (0, 2): 0, (2, 0): 2, (1, 1): 2, (3, 1): 1, (3, 3): 3,
          (1, 3): 2, (1, 2): 2, (2, 1): 1, (3, 2): 3, (2, 3): 2, (2, 2): 1}
STEP = ((1, 0), (0, 1), (-1, 0), (0, -1))

def tree_kids():
    kids = [[[] for _ in range(4)] for _ in range(4)]
    for node, way in WAY_IN.items():
        for q in range(4):
            x, y = node
            for _ in range(q):
                x, y = (-y) % 4, x
            e = (way + q) % 4
            kids[q][e].append((x - STEP[e][0]) % 4 + 4 * ((y - STEP[e][1]) % 4))
    return kids
KIDS = tree_kids()

def tree_depths():
    out = [[0] * 16 for _ in range(4)]
    for node in WAY_IN:
        u, k = node, 0
        while u != (0, 0):
            s = STEP[WAY_IN[u]]
            u, k = ((u[0] - s[0]) % 4, (u[1] - s[1]) % 4), k + 1
        x, y = node
        for q in range(4):
            out[q][x + 4 * y] = k
            x, y = (-y) % 4, x
    return out
DEPTH = tree_depths()


R = 8
D = 3
CH = 256 // R
DEEP = 5
PIECE = 192


def sl(a):
    h, l = split(a)
    return jnp.concatenate([h, l, h], axis=1)


def sr(b):
    h, l = split(b)
    return jnp.concatenate([h, h, l], axis=0)


def mm(left, right):
    return jnp.dot(left, right, preferred_element_type=f32)


def nt(left, right):
    return lax.dot_general(left, right, (((1,), (1,)), ((), ())), preferred_element_type=f32)


def nt3(lh, ll, rh, rl):
    return nt(lh, rh) + (nt(ll, rh) + nt(lh, rl))


def kernel(prior, coords_t, coords, carried, target, scal, u_out, w_out,
           head, ph, plo, hh, hl, part, sib, zr, full, wbuf, stage, xyh, pj,
           head_send, head_recv, w_send, w_recv, ws_send, ws_recv, x_send, x_recv,
           j_send, j_recv, p_send, p_recv, st_sem, o_sem):
    x, y, d = lax.axis_index("col"), lax.axis_index("row"), lax.axis_index("depth")
    z, core = lax.div(d, 2), lax.rem(d, 2)
    node = x + 4 * y
    nbr = [{"col": lax.rem(x + 4 + sx, 4), "row": lax.rem(y + 4 + sy, 4)} for sx, sy in STEP]
    sibling = {"depth": 2 * z + 1 - core}
    is_root = node == 0

    def zpeer(k):
        return {"depth": 2 * lax.rem(z + k, 4) + core}

    def remote(src, dst, ss, rs, dev):
        return pltpu.make_async_remote_copy(
            src_ref=src, dst_ref=dst, send_sem=ss, recv_sem=rs, device_id=dev, device_id_type=MESH)

    sends = {}
    for q in range(4):
        for e in range(4):
            if KIDS[q][e]:
                sends[q, e] = functools.reduce(jnp.logical_or, [node == k for k in KIDS[q][e]])
    depth = [sum(jnp.where(node == v, DEPTH[q][v], 0) for v in range(1, 16)) for q in range(4)]

    barrier = pltpu.get_barrier_semaphore()
    for e in range(4):
        pl.semaphore_signal(barrier, inc=1, device_id=nbr[e], device_id_type=MESH)
    for k in range(1, 8):
        pl.semaphore_signal(barrier, inc=1, device_id={"depth": lax.rem(d + k, 8)}, device_id_type=MESH)
    pl.semaphore_wait(barrier, 11)

    def hrows(q, c):
        return pl.ds(pl.multiple_of((c * 4 + q) * R, R), R)

    def hcopy(q, e, c, src):
        return remote(src.at[hrows(q, c)], head.at[hrows(q, c)], head_send.at[q, e], head_recv.at[q, c], nbr[e])

    def wrows(q, k, cr):
        return pl.ds(pl.multiple_of(k * B + cr * 64 + q * 16, 16), 16)

    def wcopy(q, e, k):
        r = wrows(q, k, core)
        return remote(wbuf.at[r], wbuf.at[r], w_send.at[q, e], w_recv.at[q, k], nbr[e])

    def wsib(q, k, cr):
        r = wrows(q, k, cr)
        return remote(wbuf.at[r], wbuf.at[r], ws_send, ws_recv.at[q, k], sibling)

    def xcopy(e, i):
        ref = xyh if i == 0 else wbuf.at[pl.ds(1024, 8)]
        return remote(ref, ref, x_send.at[i, e], x_recv.at[i], nbr[e])

    def forward(q, start):
        for e in range(4):
            if (q, e) in sends and any(k != 0 for k in KIDS[q][e]):
                @pl.when(sends[q, e])
                def _():
                    start(e)

    def root_send(q, start):
        for e in range(4):
            if (q, e) in sends and 0 in KIDS[q][e]:
                start(e)

    def arrive(s):
        for q in range(4):
            c = s - D * (depth[q] - 1)

            @pl.when((c >= 0) & (c < CH))
            def _():
                hcopy(q, 0, c, head).wait_recv()
                forward(q, lambda e: hcopy(q, e, c, head).start())
            if q == 0:
                @pl.when(c == 1)
                def _():
                    xcopy(0, 0).wait_recv()
                    forward(0, lambda e: xcopy(e, 0).start())

    def w_round(k0, n):
        def body(t, _):
            for q in range(4):
                k = k0 + t - (depth[q] - 1)

                @pl.when((k >= k0) & (k < k0 + n))
                def _():
                    wcopy(q, 0, k).wait_recv()
                    forward(q, lambda e: wcopy(q, e, k).start())
                    wsib(q, k, core).start()
            return 0
        lax.fori_loop(0, n + DEEP - 1, body, 0)

    def load(i, slot):
        rows = pl.ds(pl.multiple_of(i * PIECE, PIECE), PIECE)
        return pltpu.make_async_copy(prior.at[rows], stage.at[slot], st_sem.at[slot])

    def take(i):
        slot = lax.rem(i, 2)
        load(i, slot).wait()
        for t in range(0, PIECE, 16):
            h, l = split(stage[slot, t:t + 16, :])
            rows = pl.ds(pl.multiple_of(i * PIECE + t, 16), 16)
            ph[rows, :] = h
            plo[rows, :] = l

        @pl.when(i + 2 < 8)
        def _():
            load(i + 2, slot).start()

    def spot(job):
        cols, rb, s, so, zo, j = job
        return pl.ds(cols[0], cols[1]), rb, s, so, zo, j

    def own(job, zz, cr):
        _, rb, s, _, _, _ = job
        return pl.ds(pl.multiple_of(rb + cr * 4 * s + zz * s, 16), s)

    def a_copy(job):
        cols, rb, s, so, zo, j = spot(job)
        return remote(part.at[pl.ds(pl.multiple_of(rb + (1 - core) * 4 * s, 16), 4 * s), cols],
                      sib.at[pl.ds(so, 4 * s), cols], j_send.at[j, 0], j_recv.at[j, 0], sibling)

    def b_copy(job, k):
        cols, rb, s, so, zo, j = spot(job)
        return remote(part.at[own(job, lax.rem(z + k, 4), core), cols],
                      zr.at[k - 1, pl.ds(zo, s), cols], j_send.at[j, k], j_recv.at[j, k], zpeer(k))

    def c_copy(job, k):
        cols, rb, s, so, zo, j = spot(job)
        o = own(job, z, core)
        return remote(full.at[o, cols], full.at[o, cols], j_send.at[j, 3 + k], j_recv.at[j, 3 + k],
                      zpeer(k) if k < 4 else sibling)

    def d_copy(job, k, cr):
        cols, rb, s, so, zo, j = spot(job)
        o = own(job, lax.rem(z + 4 - k, 4), cr)
        return remote(full.at[o, cols], full.at[o, cols], j_send.at[j, 7 + k], j_recv.at[j, 7 + k], sibling)

    def step_a(job):
        a_copy(job).start()

    def step_b(job):
        cols, rb, s, so, zo, j = spot(job)
        a_copy(job).wait_recv()

        def body(i, _):
            o = pl.ds(pl.multiple_of(rb + core * 4 * s + i * 32, 32), 32)
            part[o, cols] = part[o, cols] + sib[pl.ds(pl.multiple_of(so + i * 32, 32), 32), cols]
            return 0
        lax.fori_loop(0, s // 8, body, 0)
        for k in (2, 1, 3):
            b_copy(job, k).start()

    def step_c(job, nugget):
        cols, rb, s, so, zo, j = spot(job)
        wide = job[0][1]
        for k in (1, 2, 3):
            b_copy(job, k).wait_recv()
        hx, hy = xyh[0:1, cols], xyh[1:2, cols]

        def body(i, _):
            first = rb + core * 4 * s + z * s + i * 32
            o = pl.ds(pl.multiple_of(first, 32), 32)
            t = pl.ds(pl.multiple_of(zo + i * 32, 32), 32)
            total = part[o, cols] + zr[0, t, cols] + (zr[1, t, cols] + zr[2, t, cols])
            dx = coords_t[o, 0:1] - hx
            dy = coords_t[o, 1:2] - hy
            scaled = root_three * jnp.sqrt(dx * dx + dy * dy) / scal[1]
            val = scal[0] * (1.0 + scaled) * jnp.exp(-scaled)
            if nugget:
                ri = lax.broadcasted_iota(jnp.int32, (32, wide), 0) + first
                ci = lax.broadcasted_iota(jnp.int32, (32, wide), 1) + job[0][0]
                val = val + jnp.where(ri == ci, scal[2], 0.0)
            full[o, cols] = val - total
            return 0
        lax.fori_loop(0, s // 32, body, 0)
        for k in (2, 1, 3, 4):
            c_copy(job, k).start()

    def step_d(job):
        for k in (1, 3, 2):
            c_copy(job, k).wait_recv()
            d_copy(job, k, core).start()

    def step_e(job):
        c_copy(job, 4).wait_recv()
        for k in (1, 2, 3):
            d_copy(job, k, 1 - core).wait_recv()

    def job_done(job):
        a_copy(job).wait_send()
        for k in (1, 2, 3):
            b_copy(job, k).wait_send()
            c_copy(job, k).wait_send()
            d_copy(job, k, core).wait_send()
        c_copy(job, 4).wait_send()

    load(0, 0).start()
    load(1, 1).start()

    @pl.when(is_root)
    def _():
        xyh[0:2, :] = coords[:, 0:1024]

        def send(c, _):
            for q in range(4):
                root_send(q, lambda e: hcopy(q, e, c, prior).start())

            @pl.when(c == 1)
            def _():
                root_send(0, lambda e: xcopy(e, 0).start())
            return 0
        lax.fori_loop(0, CH, send, 0)

        def tk(i, _):
            take(i)
            return 0
        lax.fori_loop(0, 8, tk, 0)
        gram = [((256 * c, 256), 256 * c, 32 * (4 - c), 0, 0, c) for c in range(4)]
        rest = ((0, 1024), 1024, 64, 512, 128, 4)

        def blk(rb, c):
            r = pl.ds(pl.multiple_of(rb * 256, 256), 256)
            cc = pl.ds(pl.multiple_of(c * 256, 256), 256)
            part[r, cc] = nt3(ph[r, :], plo[r, :], ph[cc, :], plo[cc, :])
        for c in range(4):
            def body(rb, _):
                blk(rb, c)
                return 0
            lax.fori_loop(c, 4, body, 0)
            step_a(gram[c])
            if c:
                step_b(gram[c - 1])
        step_b(gram[3])
        ch, cl = split(jnp.broadcast_to(carried[...], (16, 2048)))

        def pbody(c, _):
            cc = pl.ds(pl.multiple_of(c * 256, 256), 256)
            pj[0, :, cc] = nt3(ch, cl, ph[cc, :], plo[cc, :])[0:8]
            return 0
        lax.fori_loop(0, 4, pbody, 0)

        def pcopy(k):
            return remote(pj.at[0], pj.at[k], p_send.at[k - 1], p_recv.at[k - 1], {"depth": lax.rem(d + k, 8)})
        for k in range(1, 8):
            pcopy(k).start()
        step_c(gram[0], True)
        step_c(gram[1], True)

        def rbody(i, _):
            blk(4 + lax.div(i, 4), lax.rem(i, 4))
            return 0
        lax.fori_loop(0, 8, rbody, 0)
        step_a(rest)
        step_d(gram[0])
        step_c(gram[2], True)
        n = 1024
        head[:, 0:n] = jnp.zeros((n, n), f32)

        def merge(c):
            step_e(gram[c])
            lo, hi = 256 * c, 256 * c + 256
            head[lo:n, lo:hi] = head[lo:n, lo:hi] + full[lo:n, lo:hi]
            if c < 3:
                t = full[hi:n, lo:hi].T
                head[lo:hi, hi:n] = head[lo:hi, hi:n] + t
                full[lo:hi, hi:n] = t
        merge(0)
        ri = lax.broadcasted_iota(jnp.int32, (B, n), 0)
        ci = lax.broadcasted_iota(jnp.int32, (B, n), 1)
        rows = lax.broadcasted_iota(jnp.int32, (n, 1), 0)

        def step(k, _):
            @pl.when(k == 1)
            def _():
                step_d(gram[1])
                step_c(gram[3], True)

            @pl.when(k == 2)
            def _():
                merge(1)
                step_d(gram[2])

            @pl.when(k == 3)
            def _():
                step_d(gram[3])
                step_b(rest)

            @pl.when(k == 4)
            def _():
                merge(2)

            @pl.when(k == 5)
            def _():
                step_c(rest, False)

            @pl.when(k == 6)
            def _():
                merge(3)

            @pl.when(k == 7)
            def _():
                step_d(rest)
            ks = pl.multiple_of(k * B, B)
            m = base(head[pl.ds(ks, B), pl.ds(ks, B)])
            inblk = (ci >= ks) & (ci < ks + B)
            row = jnp.where(inblk, (ci == ri + ks).astype(f32), head[pl.ds(ks, B), 0:n])
            r = mm(sl(m), sr(row))
            wbuf[pl.ds(ks, B), :] = jnp.where(ci < ks + B, r, 0.0)
            for q in range(4):
                root_send(q, lambda e: wcopy(q, e, k).start())
            rs = sr(r)
            mt = sr(m.T)
            act = rows >= ks + B
            gs = sl(jnp.where(act, mm(sl(head[:, pl.ds(ks, B)]), mt), 0.0))
            for i in range(1, 8):
                zap = act[i * B:(i + 1) * B] & inblk
                cur = jnp.where(zap, 0.0, head[i * B:(i + 1) * B, 0:n])
                head[i * B:(i + 1) * B, 0:n] = cur - mm(gs[i * B:(i + 1) * B], rs)
            return 0
        lax.fori_loop(0, 8, step, 0)
        for k in range(1, 8):
            pcopy(k).wait_recv()
        proj = functools.reduce(jnp.add, [pj[k] for k in range(8)])
        rh, rl = split(jnp.concatenate([target[...] - proj] * 2, axis=0))

        def sbody(i, _):
            cc = pl.ds(pl.multiple_of(i * 256, 256), 256)
            wh, wl = split(wbuf[cc, :])
            wbuf[1024:1032, cc] = nt3(rh, rl, wh, wl)[0:8]
            return 0
        lax.fori_loop(0, 4, sbody, 0)
        root_send(0, lambda e: xcopy(e, 1).start())
        step_e(rest)
        for job in gram + [rest]:
            job_done(job)
        for k in range(1, 8):
            pcopy(k).wait_send()

    @pl.when(jnp.logical_not(is_root))
    def _():
        jobs = [((256 * c, 256), 0, 192, 0, 0, c) for c in range(4)]

        def early(s, _):
            arrive(s)
            take(s)
            return 0
        lax.fori_loop(0, 8, early, 0)
        lead = 8 + D * (DEEP - 1)

        def wait_only(s, _):
            arrive(s)
            return 0
        lax.fori_loop(8, lead, wait_only, 0)

        def block(m, with_arrivals):
            for t in range(0, 256, 16):
                h, l = split(head[pl.ds(pl.multiple_of(m * 256 + t, 16), 16), :])
                hh[t:t + 16, :] = h
                hl[t:t + 16, :] = l

            def piece(i, _):
                if with_arrivals:
                    arrive(lead + 8 * m + i)
                r = pl.ds(pl.multiple_of(i * PIECE, PIECE), PIECE)
                part[r, pl.ds(pl.multiple_of(m * 256, 256), 256)] = nt3(ph[r, :], plo[r, :], hh[...], hl[...])
                return 0
            lax.fori_loop(0, 8, piece, 0)
        block(0, True)
        step_a(jobs[0])
        block(1, True)
        step_a(jobs[1])
        step_b(jobs[0])
        block(2, True)
        step_a(jobs[2])
        step_b(jobs[1])
        step_c(jobs[0], False)
        block(3, False)
        step_a(jobs[3])
        step_b(jobs[2])
        step_c(jobs[1], False)
        step_d(jobs[0])
        step_b(jobs[3])
        step_c(jobs[2], False)
        step_d(jobs[1])
        w_round(0, 4)
        step_c(jobs[3], False)
        step_d(jobs[2])
        w_round(4, 3)
        step_d(jobs[3])
        for c in range(4):
            step_e(jobs[c])
        w_round(7, 1)
        xcopy(0, 1).wait_recv()
        forward(0, lambda e: xcopy(e, 1).start())
        for q in range(4):
            for k in range(8):
                wsib(q, k, 1 - core).wait_recv()
        for job in jobs:
            job_done(job)
        whole = wbuf.at[pl.ds(0, 512)]
        remote(whole, whole, ws_send, ws_recv.at[0, 0], sibling).wait_send()

    ucp = pltpu.make_async_copy(full, u_out, o_sem.at[0])
    wcp = pltpu.make_async_copy(wbuf, w_out, o_sem.at[1])
    ucp.start()
    wcp.start()
    for (q, e), has in sends.items():
        @pl.when(has)
        def _():
            ref = head.at[pl.ds(0, 256)]
            remote(ref, ref, head_send.at[q, e], head_recv.at[0, 0], nbr[e]).wait_send()
            ref = wbuf.at[pl.ds(0, 128)]
            remote(ref, ref, w_send.at[q, e], w_recv.at[0, 0], nbr[e]).wait_send()
            if q == 0:
                xcopy(e, 0).wait_send()
                xcopy(e, 1).wait_send()
    ucp.wait()
    wcp.wait()


def gather_and_factor(prior, coords, carried, target, scal):
    vm = pl.BlockSpec(memory_space=pltpu.VMEM)
    dma = pltpu.SemaphoreType.DMA
    bf = jnp.bfloat16
    return pl.pallas_call(
        kernel,
        out_shape=(jax.ShapeDtypeStruct((1536, 1024), f32), jax.ShapeDtypeStruct((1032, 1024), f32)),
        in_specs=[pl.BlockSpec(memory_space=pl.ANY), vm, vm, vm, vm, pl.BlockSpec(memory_space=pltpu.SMEM)],
        out_specs=(pl.BlockSpec(memory_space=pl.ANY), pl.BlockSpec(memory_space=pl.ANY)),
        scratch_shapes=[
            pltpu.VMEM((1024, 2048), f32),
            pltpu.VMEM((1536, 2048), bf), pltpu.VMEM((1536, 2048), bf),
            pltpu.VMEM((256, 2048), bf), pltpu.VMEM((256, 2048), bf),
            pltpu.VMEM((1536, 1024), f32), pltpu.VMEM((768, 1024), f32), pltpu.VMEM((3, 192, 1024), f32),
            pltpu.VMEM((1536, 1024), f32), pltpu.VMEM((1032, 1024), f32), pltpu.VMEM((2, PIECE, 2048), f32),
            pltpu.VMEM((8, 1024), f32), pltpu.VMEM((8, 8, 1024), f32),
            dma((4, 4)), dma((4, CH)), dma((4, 4)), dma((4, 8)), dma, dma((4, 8)), dma((2, 4)), dma((2,)),
            dma((5, 11)), dma((5, 11)), dma((7,)), dma((7,)), dma((2,)), dma((2,)),
        ],
        compiler_params=pltpu.CompilerParams(collective_id=1, has_side_effects=True, vmem_limit_bytes=60 << 20),
    )(prior, coords.T, coords, carried[None, :], target[None, :], scal)


def local(coords, prior, target, carried, variance, lengthscale, nugget):
    scal = jnp.concatenate([variance, lengthscale, nugget])
    update, inverse = gather_and_factor(prior, coords, carried, target, scal)
    panels = jnp.einsum("rk,ck->rc", update, inverse[:1024], precision=lax.Precision.HIGH)
    return (panels, inverse[1024])


def solution(mesh):
    return jax.shard_map(
        local,
        mesh=mesh,
        in_specs=(
            P(None, ("row", "col")),
            P(("row", "col"), "depth"),
            P(),
            P("depth"),
            P(),
            P(),
            P(),
        ),
        out_specs=(P(("row", "col"), None), P()),
        check_vma=False,
    )
```

time: 326 us -> 191 us (0.59)
  the two profiles are of different devices: /device:TPU:1 before, /device:TPU:50 now
where the time goes in v2:
time: 191 us
  Pallas kernels  170 us (89%)
  matrix products  14.7 us (8%)
  local copies, waits for them, and re-layouts  3.23 us (2%)
  between operations  2.58 us (1%)
    pallas_call x1, Pallas kernels, gather_and_factor(): pl.pallas_call(kernel, out_shape=(jax.ShapeDtypeStruct((1536, 1024), f32)...  170 us
    dot_general x1, matrix products, local(): jnp.einsum('rk,ck->rc', update, inverse[:1024], precision=lax.Precision.H...  14.7 us

profile of v2, /device:TPU:50, one launch (start us, length us, event | category | flops | bytes accessed | tf_op | source)
XLA Modules:
  0.0 190.7 jit_solution(655191798900228607)
XLA Ops:
  2.6 0.6 pad_maximum_fusion.scal
  3.2 1.9 copy.9
  5.0 169.7 %shard_map.86 = (f32[1536,1024]{1,0:T(8,128)}, f32[1032,1024]{1,0:T(8,128)}) custom-call(f32[1536,2048]{1,0:T(8,128)} %prior.1, f32[1536,2]{1,0:T(8,128)} %bitcast.5, f32[2,1536]{1,0:T(2,128)} %coords.1, f32[1,2048]{1,0:T(1,128)} %bitcast.6, f32[1,1024]{1,0:T(1,128)} %bitcast.7, f32[3]{0:T(128)} %pad_maximum_fusion.scal), custom_call_target="tpu_custom_call" | custom-call | tf_op jit(solution)/shard_map/pallas_call | solution.py:555
  174.7 14.7 %fusion = f32[1536,1024]{1,0:T(8,128)} fusion(f32[1536,1024]{1,0:T(8,128)} %get-tuple-element.4, f32[1032,1024]{1,0:T(8,128)} %get-tuple-element.5), kind=kOutput, calls=%fused_computation | convolution fusion | flops 9663676416 | bytes 16777216 | tf_op jit(solution)/shard_map/rk,ck->rc/dot_general | solution.py:577
  189.4 1.4 slice.7

commit v3 on v2

--- a/solution.py
+++ b/solution.py
@@ -127,8 +127,8 @@
     return nt(lh, rh) + (nt(ll, rh) + nt(lh, rl))
 
 
-def kernel(prior, coords_t, coords, carried, target, scal, u_out, w_out,
-           head, ph, plo, hh, hl, part, sib, zr, full, wbuf, stage, xyh, pj,
+def kernel(prior, coords, carried, target, variance, lengthscale, nugget_ref, u_out, w_out,
+           coords_t, head, ph, plo, hh, hl, part, sib, zr, full, wbuf, stage, xyh, pj,
            head_send, head_recv, w_send, w_recv, ws_send, ws_recv, x_send, x_recv,
            j_send, j_recv, p_send, p_recv, st_sem, o_sem):
     x, y, d = lax.axis_index("col"), lax.axis_index("row"), lax.axis_index("depth")
@@ -206,18 +206,26 @@
                     xcopy(0, 0).wait_recv()
                     forward(0, lambda e: xcopy(e, 0).start())
 
-    def w_round(k0, n):
+    def w_hop(k0, n, t):
+        for q in range(4):
+            k = k0 + t - (depth[q] - 1)
+
+            @pl.when((k >= k0) & (k < k0 + n))
+            def _():
+                wcopy(q, 0, k).wait_recv()
+                forward(q, lambda e: wcopy(q, e, k).start())
+                wsib(q, k, core).start()
+            if k0 == 0 and q == 0:
+                @pl.when(k == 1)
+                def _():
+                    xcopy(0, 1).wait_recv()
+                    forward(0, lambda e: xcopy(e, 1).start())
+
+    def w_hops(k0, n, lo, hi):
         def body(t, _):
-            for q in range(4):
-                k = k0 + t - (depth[q] - 1)
-
-                @pl.when((k >= k0) & (k < k0 + n))
-                def _():
-                    wcopy(q, 0, k).wait_recv()
-                    forward(q, lambda e: wcopy(q, e, k).start())
-                    wsib(q, k, core).start()
-            return 0
-        lax.fori_loop(0, n + DEEP - 1, body, 0)
+            w_hop(k0, n, t)
+            return 0
+        lax.fori_loop(lo, hi, body, 0)
 
     def load(i, slot):
         rows = pl.ds(pl.multiple_of(i * PIECE, PIECE), PIECE)
@@ -265,6 +273,18 @@
         o = own(job, lax.rem(z + 4 - k, 4), cr)
         return remote(full.at[o, cols], full.at[o, cols], j_send.at[j, 7 + k], j_recv.at[j, 7 + k], sibling)
 
+    def h_copy(job, half, zz, cr, dev, idx):
+        cols, rb, s, so, zo, j = spot(job)
+        o = pl.ds(pl.multiple_of(rb + cr * 4 * s + zz * s + half * (s // 2), 8), s // 2)
+        return remote(full.at[o, cols], full.at[o, cols], j_send.at[j, idx], j_recv.at[j, idx], dev)
+
+    def across(job, half):
+        zz = lax.rem(z + (3 if half == 0 else 1), 4)
+        return h_copy(job, half, zz, core, zpeer(1 if half == 0 else 3), 11 + half)
+
+    def beside(job, half):
+        return h_copy(job, half, lax.rem(z + 2, 4), core, sibling, 13 + half)
+
     def step_a(job):
         a_copy(job).start()
 
@@ -280,7 +300,7 @@
         for k in (2, 1, 3):
             b_copy(job, k).start()
 
-    def step_c(job, nugget):
+    def step_c(job, nugget, relay=False):
         cols, rb, s, so, zo, j = spot(job)
         wide = job[0][1]
         for k in (1, 2, 3):
@@ -294,38 +314,54 @@
             total = part[o, cols] + zr[0, t, cols] + (zr[1, t, cols] + zr[2, t, cols])
             dx = coords_t[o, 0:1] - hx
             dy = coords_t[o, 1:2] - hy
-            scaled = root_three * jnp.sqrt(dx * dx + dy * dy) / scal[1]
-            val = scal[0] * (1.0 + scaled) * jnp.exp(-scaled)
+            scaled = root_three * jnp.sqrt(dx * dx + dy * dy) / lengthscale[0]
+            val = variance[0] * (1.0 + scaled) * jnp.exp(-scaled)
             if nugget:
                 ri = lax.broadcasted_iota(jnp.int32, (32, wide), 0) + first
                 ci = lax.broadcasted_iota(jnp.int32, (32, wide), 1) + job[0][0]
-                val = val + jnp.where(ri == ci, scal[2], 0.0)
+                val = val + jnp.where(ri == ci, nugget_ref[0], 0.0)
             full[o, cols] = val - total
             return 0
         lax.fori_loop(0, s // 32, body, 0)
-        for k in (2, 1, 3, 4):
+        for k in (1, 3, 4) if relay else (2, 1, 3, 4):
             c_copy(job, k).start()
 
-    def step_d(job):
-        for k in (1, 3, 2):
+    def step_d(job, relay=False):
+        for k in (1, 3) if relay else (1, 3, 2):
             c_copy(job, k).wait_recv()
+            if relay:
+                across(job, 0 if k == 1 else 1).start()
             d_copy(job, k, core).start()
 
-    def step_e(job):
+    def step_f(job):
+        for half in (0, 1):
+            across(job, half).wait_recv()
+            beside(job, half).start()
+
+    def step_e(job, relay=False):
         c_copy(job, 4).wait_recv()
-        for k in (1, 2, 3):
+        for k in (1, 3) if relay else (1, 2, 3):
             d_copy(job, k, 1 - core).wait_recv()
-
-    def job_done(job):
+        if relay:
+            for half in (0, 1):
+                beside(job, half).wait_recv()
+
+    def job_done(job, relay=False):
         a_copy(job).wait_send()
         for k in (1, 2, 3):
             b_copy(job, k).wait_send()
-            c_copy(job, k).wait_send()
-            d_copy(job, k, core).wait_send()
+            if k != 2 or not relay:
+                c_copy(job, k).wait_send()
+                d_copy(job, k, core).wait_send()
         c_copy(job, 4).wait_send()
+        if relay:
+            for half in (0, 1):
+                across(job, half).wait_send()
+                beside(job, half).wait_send()
 
     load(0, 0).start()
     load(1, 1).start()
+    coords_t[...] = jnp.concatenate([coords[...]] * 4, axis=0).T
 
     @pl.when(is_root)
     def _():
@@ -348,19 +384,16 @@
         gram = [((256 * c, 256), 256 * c, 32 * (4 - c), 0, 0, c) for c in range(4)]
         rest = ((0, 1024), 1024, 64, 512, 128, 4)
 
-        def blk(rb, c):
-            r = pl.ds(pl.multiple_of(rb * 256, 256), 256)
+        def blk(rb, n, c):
             cc = pl.ds(pl.multiple_of(c * 256, 256), 256)
-            part[r, cc] = nt3(ph[r, :], plo[r, :], ph[cc, :], plo[cc, :])
+            part[rb:rb + n, cc] = nt3(ph[rb:rb + n, :], plo[rb:rb + n, :], ph[cc, :], plo[cc, :])
         for c in range(4):
-            def body(rb, _):
-                blk(rb, c)
-                return 0
-            lax.fori_loop(c, 4, body, 0)
+            blk(256 * c, 1024 - 256 * c, c)
             step_a(gram[c])
             if c:
                 step_b(gram[c - 1])
         step_b(gram[3])
+        step_c(gram[0], True)
         ch, cl = split(jnp.broadcast_to(carried[...], (16, 2048)))
 
         def pbody(c, _):
@@ -373,15 +406,17 @@
             return remote(pj.at[0], pj.at[k], p_send.at[k - 1], p_recv.at[k - 1], {"depth": lax.rem(d + k, 8)})
         for k in range(1, 8):
             pcopy(k).start()
-        step_c(gram[0], True)
         step_c(gram[1], True)
 
         def rbody(i, _):
-            blk(4 + lax.div(i, 4), lax.rem(i, 4))
-            return 0
-        lax.fori_loop(0, 8, rbody, 0)
+            r = pl.ds(pl.multiple_of(1024 + lax.div(i, 4) * 256, 256), 256)
+            cc = pl.ds(pl.multiple_of(lax.rem(i, 4) * 256, 256), 256)
+            part[r, cc] = nt3(ph[r, :], plo[r, :], ph[cc, :], plo[cc, :])
+            return 0
+        lax.fori_loop(0, 4, rbody, 0)
+        step_d(gram[0])
+        lax.fori_loop(4, 8, rbody, 0)
         step_a(rest)
-        step_d(gram[0])
         step_c(gram[2], True)
         n = 1024
         head[:, 0:n] = jnp.zeros((n, n), f32)
@@ -414,6 +449,11 @@
             def _():
                 step_d(gram[3])
                 step_b(rest)
+                for i in range(1, 8):
+                    pcopy(i).wait_recv()
+                proj = functools.reduce(jnp.add, [pj[i] for i in range(8)])
+                wbuf[1024:1032, :] = target[...] - proj
+                root_send(0, lambda e: xcopy(e, 1).start())
 
             @pl.when(k == 4)
             def _():
@@ -438,28 +478,20 @@
             wbuf[pl.ds(ks, B), :] = jnp.where(ci < ks + B, r, 0.0)
             for q in range(4):
                 root_send(q, lambda e: wcopy(q, e, k).start())
-            rs = sr(r)
-            mt = sr(m.T)
-            act = rows >= ks + B
-            gs = sl(jnp.where(act, mm(sl(head[:, pl.ds(ks, B)]), mt), 0.0))
-            for i in range(1, 8):
-                zap = act[i * B:(i + 1) * B] & inblk
-                cur = jnp.where(zap, 0.0, head[i * B:(i + 1) * B, 0:n])
-                head[i * B:(i + 1) * B, 0:n] = cur - mm(gs[i * B:(i + 1) * B], rs)
+
+            @pl.when(k < 7)
+            def _():
+                rs = sr(r)
+                mt = sr(m.T)
+                act = rows >= ks + B
+                gs = sl(jnp.where(act, mm(sl(head[:, pl.ds(ks, B)]), mt), 0.0))
+                for i in range(1, 8):
+                    zap = act[i * B:(i + 1) * B] & inblk
+                    cur = jnp.where(zap, 0.0, head[i * B:(i + 1) * B, 0:n])
+                    head[i * B:(i + 1) * B, 0:n] = cur - mm(gs[i * B:(i + 1) * B], rs)
             return 0
         lax.fori_loop(0, 8, step, 0)
-        for k in range(1, 8):
-            pcopy(k).wait_recv()
-        proj = functools.reduce(jnp.add, [pj[k] for k in range(8)])
-        rh, rl = split(jnp.concatenate([target[...] - proj] * 2, axis=0))
-
-        def sbody(i, _):
-            cc = pl.ds(pl.multiple_of(i * 256, 256), 256)
-            wh, wl = split(wbuf[cc, :])
-            wbuf[1024:1032, cc] = nt3(rh, rl, wh, wl)[0:8]
-            return 0
-        lax.fori_loop(0, 4, sbody, 0)
-        root_send(0, lambda e: xcopy(e, 1).start())
+
         step_e(rest)
         for job in gram + [rest]:
             job_done(job)
@@ -468,65 +500,71 @@
 
     @pl.when(jnp.logical_not(is_root))
     def _():
-        jobs = [((256 * c, 256), 0, 192, 0, 0, c) for c in range(4)]
+        jobs = [((128 * c, 128), 0, 192, 0, 0, c) for c in range(8)]
 
         def early(s, _):
             arrive(s)
             take(s)
             return 0
         lax.fori_loop(0, 8, early, 0)
-        lead = 8 + D * (DEEP - 1)
+        lead = 4 + D * (DEEP - 1)
 
         def wait_only(s, _):
             arrive(s)
             return 0
         lax.fori_loop(8, lead, wait_only, 0)
 
-        def block(m, with_arrivals):
-            for t in range(0, 256, 16):
-                h, l = split(head[pl.ds(pl.multiple_of(m * 256 + t, 16), 16), :])
-                hh[t:t + 16, :] = h
-                hl[t:t + 16, :] = l
+        def block(m, hops=None):
+            def cut(t, _):
+                h, l = split(head[pl.ds(pl.multiple_of(m * 128 + t * 16, 16), 16), :])
+                o = pl.ds(pl.multiple_of(t * 16, 16), 16)
+                hh[o, :] = h
+                hl[o, :] = l
+                return 0
+            lax.fori_loop(0, 8, cut, 0)
 
             def piece(i, _):
-                if with_arrivals:
-                    arrive(lead + 8 * m + i)
-                r = pl.ds(pl.multiple_of(i * PIECE, PIECE), PIECE)
-                part[r, pl.ds(pl.multiple_of(m * 256, 256), 256)] = nt3(ph[r, :], plo[r, :], hh[...], hl[...])
+                if m < 7:
+                    arrive(lead + 4 * m + i)
+                r = pl.ds(pl.multiple_of(i * 384, 384), 384)
+                part[r, m * 128:m * 128 + 128] = nt3(ph[r, :], plo[r, :], hh[...], hl[...])
+                if hops is not None:
+                    @pl.when(lax.rem(i, 2) == 1)
+                    def _():
+                        w_hop(0, 4, hops + lax.div(i, 2))
                 return 0
-            lax.fori_loop(0, 8, piece, 0)
-        block(0, True)
-        step_a(jobs[0])
-        block(1, True)
-        step_a(jobs[1])
-        step_b(jobs[0])
-        block(2, True)
-        step_a(jobs[2])
-        step_b(jobs[1])
-        step_c(jobs[0], False)
-        block(3, False)
-        step_a(jobs[3])
-        step_b(jobs[2])
-        step_c(jobs[1], False)
-        step_d(jobs[0])
-        step_b(jobs[3])
-        step_c(jobs[2], False)
-        step_d(jobs[1])
-        w_round(0, 4)
-        step_c(jobs[3], False)
-        step_d(jobs[2])
-        w_round(4, 3)
-        step_d(jobs[3])
-        for c in range(4):
-            step_e(jobs[c])
-        w_round(7, 1)
-        xcopy(0, 1).wait_recv()
-        forward(0, lambda e: xcopy(e, 1).start())
+            lax.fori_loop(0, 4, piece, 0)
+
+        def tick(t):
+            if t < 8:
+                step_a(jobs[t])
+            if 0 <= t - 1 < 8:
+                step_b(jobs[t - 1])
+            if 0 <= t - 2 < 8:
+                step_c(jobs[t - 2], False, True)
+            if 0 <= t - 3 < 8:
+                step_d(jobs[t - 3], True)
+            if 0 <= t - 4 < 8:
+                step_f(jobs[t - 4])
+        for m in range(8):
+            block(m, 2 * (m - 5) if m >= 5 else None)
+            tick(m)
+        w_hops(0, 4, 6, 8)
+        tick(8)
+        w_hops(4, 4, 0, 3)
+        tick(9)
+        w_hops(4, 4, 3, 5)
+        tick(10)
+        w_hops(4, 4, 5, 7)
+        tick(11)
+        w_hops(4, 4, 7, 8)
+        for c in range(8):
+            step_e(jobs[c], True)
         for q in range(4):
             for k in range(8):
                 wsib(q, k, 1 - core).wait_recv()
         for job in jobs:
-            job_done(job)
+            job_done(job, True)
         whole = wbuf.at[pl.ds(0, 512)]
         remote(whole, whole, ws_send, ws_recv.at[0, 0], sibling).wait_send()
 
@@ -548,34 +586,68 @@
     wcp.wait()
 
 
-def gather_and_factor(prior, coords, carried, target, scal):
+def gather_and_factor(prior, coords, carried, target, scalars):
     vm = pl.BlockSpec(memory_space=pltpu.VMEM)
+    sm = pl.BlockSpec(memory_space=pltpu.SMEM)
     dma = pltpu.SemaphoreType.DMA
     bf = jnp.bfloat16
     return pl.pallas_call(
         kernel,
         out_shape=(jax.ShapeDtypeStruct((1536, 1024), f32), jax.ShapeDtypeStruct((1032, 1024), f32)),
-        in_specs=[pl.BlockSpec(memory_space=pl.ANY), vm, vm, vm, vm, pl.BlockSpec(memory_space=pltpu.SMEM)],
+        in_specs=[pl.BlockSpec(memory_space=pl.ANY), vm, vm, vm, sm, sm, sm],
         out_specs=(pl.BlockSpec(memory_space=pl.ANY), pl.BlockSpec(memory_space=pl.ANY)),
         scratch_shapes=[
+            pltpu.VMEM((1536, 8), f32),
             pltpu.VMEM((1024, 2048), f32),
             pltpu.VMEM((1536, 2048), bf), pltpu.VMEM((1536, 2048), bf),
-            pltpu.VMEM((256, 2048), bf), pltpu.VMEM((256, 2048), bf),
+            pltpu.VMEM((128, 2048), bf), pltpu.VMEM((128, 2048), bf),
             pltpu.VMEM((1536, 1024), f32), pltpu.VMEM((768, 1024), f32), pltpu.VMEM((3, 192, 1024), f32),
             pltpu.VMEM((1536, 1024), f32), pltpu.VMEM((1032, 1024), f32), pltpu.VMEM((2, PIECE, 2048), f32),
             pltpu.VMEM((8, 1024), f32), pltpu.VMEM((8, 8, 1024), f32),
             dma((4, 4)), dma((4, CH)), dma((4, 4)), dma((4, 8)), dma, dma((4, 8)), dma((2, 4)), dma((2,)),
-            dma((5, 11)), dma((5, 11)), dma((7,)), dma((7,)), dma((2,)), dma((2,)),
+            dma((8, 15)), dma((8, 15)), dma((7,)), dma((7,)), dma((2,)), dma((2,)),
         ],
         compiler_params=pltpu.CompilerParams(collective_id=1, has_side_effects=True, vmem_limit_bytes=60 << 20),
-    )(prior, coords.T, coords, carried[None, :], target[None, :], scal)
+    )(prior, coords, carried[None, :], target[None, :], *scalars)
+
+
+def panel_kernel(u, w, out, sol, wh, wl):
+    @pl.when(pl.program_id(0) == 0)
+    def _():
+        def cut(t, _):
+            o = pl.ds(pl.multiple_of(t * 16, 16), 16)
+            h, l = split(w[o, :])
+            wh[o, :] = h
+            wl[o, :] = l
+            return 0
+        lax.fori_loop(0, 64, cut, 0)
+        rh, rl = split(jnp.concatenate([w[1024:1032, :]] * 2, axis=0))
+        for j in range(4):
+            o = slice(256 * j, 256 * j + 256)
+            sol[:, o] = nt3(rh, rl, wh[o, :], wl[o, :])[0:1]
+    uh, ul = split(u[...])
+    for j in range(4):
+        o, n = slice(256 * j, 256 * j + 256), 256 * j + 256
+        out[:, o] = nt3(uh[:, :n], ul[:, :n], wh[o, :n], wl[o, :n])
+
+
+def panel_product(update, inverse):
+    m = 384
+    return pl.pallas_call(
+        panel_kernel,
+        grid=(1536 // m,),
+        out_shape=(jax.ShapeDtypeStruct((1536, 1024), f32), jax.ShapeDtypeStruct((1, 1024), f32)),
+        in_specs=[pl.BlockSpec((m, 1024), lambda i: (i, 0)), pl.BlockSpec((1032, 1024), lambda i: (0, 0))],
+        out_specs=(pl.BlockSpec((m, 1024), lambda i: (i, 0)), pl.BlockSpec((1, 1024), lambda i: (0, 0))),
+        scratch_shapes=[pltpu.VMEM((1024, 1024), jnp.bfloat16)] * 2,
+        compiler_params=pltpu.CompilerParams(vmem_limit_bytes=48 << 20),
+    )(update, inverse)
 
 
 def local(coords, prior, target, carried, variance, lengthscale, nugget):
-    scal = jnp.concatenate([variance, lengthscale, nugget])
-    update, inverse = gather_and_factor(prior, coords, carried, target, scal)
-    panels = jnp.einsum("rk,ck->rc", update, inverse[:1024], precision=lax.Precision.HIGH)
-    return (panels, inverse[1024])
+    update, inverse = gather_and_factor(prior, coords, carried, target, (variance, lengthscale, nugget))
+    panels, solved = panel_product(update, inverse)
+    return (panels, solved.reshape(1024))
 
 
 def solution(mesh):

time: 191 us -> 154 us (0.81)
  the two profiles are of different devices: /device:TPU:50 before, /device:TPU:13 now
where the time goes in v3:
time: 154 us; the launch traced here: 153 us
  Pallas kernels  148 us (96%)
  between operations  2.58 us (2%)
  local copies, waits for them, and re-layouts  2.19 us (1%)
    pallas_call x1, Pallas kernels, gather_and_factor(): pl.pallas_call(kernel, out_shape=(jax.ShapeDtypeStruct((1536, 1024), f32)...  136 us
    pallas_call x1, Pallas kernels, panel_product(): pl.pallas_call(panel_kernel, grid=(1536 // m,), out_shape=(jax.ShapeDtype...  12.4 us

profile of v3, /device:TPU:13, one launch (start us, length us, event | category | flops | bytes accessed | tf_op | source)
XLA Modules:
  0.0 153.3 jit_solution(8259713211764683011)
XLA Ops:
  2.6 136.1 %shard_map.86 = (f32[1536,1024]{1,0:T(8,128)}, f32[1032,1024]{1,0:T(8,128)}) custom-call(f32[1536,2048]{1,0:T(8,128)} %prior.1, f32[2,1536]{1,0:T(2,128)} %coords.1, f32[1,2048]{1,0:T(1,128)} %bitcast.3, f32[1,1024]{1,0:T(1,128)} %bitcast.4, f32[1]{0:T(128)S(6)} %copy.9.variance, f32[1]{0:T(128)S(6)} %copy.10.lengthscale, f32[1]{0:T(128)S(6)} %copy.11.nugget_ref), custom_call_target="tpu_custom_call" | custom-call | tf_op jit(solution)/shard_map/pallas_call | solution.py:594
  138.7 0.0 copy-start
  138.7 2.2 %copy-done = f32[1032,1024]{1,0:T(8,128)S(1)} copy-done((f32[1032,1024]{1,0:T(8,128)S(1)}, f32[1032,1024]{1,0:T(8,128)}, u32[]{:S(2)}) %copy-start) | copy-done | bytes 4227096
  140.9 12.4 %shard_map.87 = (f32[1536,1024]{1,0:T(8,128)}, f32[1,1024]{1,0:T(1,128)}) custom-call(f32[1536,1024]{1,0:T(8,128)} %get-tuple-element.6.u, f32[1032,1024]{1,0:T(8,128)S(1)} %copy-done), custom_call_target="tpu_custom_call" | custom-call | tf_op jit(solution)/shard_map/pallas_call | solution.py:636
Async XLA Ops:
  138.7 2.2 %copy-start = (f32[1032,1024]{1,0:T(8,128)S(1)}, f32[1032,1024]{1,0:T(8,128)}, u32[]{:S(2)}) copy-start(f32[1032,1024]{1,0:T(8,128)} %get-tuple-element.7.w) | copy-start | bytes 12681220

commit v4 on v3

--- a/solution.py
+++ b/solution.py
@@ -102,7 +102,7 @@
 D = 3
 CH = 256 // R
 DEEP = 5
-PIECE = 192
+PIECE = 96
 
 
 def sl(a):
@@ -128,7 +128,7 @@
 
 
 def kernel(prior, coords, carried, target, variance, lengthscale, nugget_ref, u_out, w_out,
-           coords_t, head, ph, plo, hh, hl, part, sib, zr, full, wbuf, stage, xyh, pj,
+           coords_t, head, ph, plo, hb, part, sib, zr, full, wbuf, stage, xyh, pj,
            head_send, head_recv, w_send, w_recv, ws_send, ws_recv, x_send, x_recv,
            j_send, j_recv, p_send, p_recv, st_sem, o_sem):
     x, y, d = lax.axis_index("col"), lax.axis_index("row"), lax.axis_index("depth")
@@ -216,7 +216,7 @@
                 forward(q, lambda e: wcopy(q, e, k).start())
                 wsib(q, k, core).start()
             if k0 == 0 and q == 0:
-                @pl.when(k == 1)
+                @pl.when(k == 3)
                 def _():
                     xcopy(0, 1).wait_recv()
                     forward(0, lambda e: xcopy(e, 1).start())
@@ -240,7 +240,7 @@
             ph[rows, :] = h
             plo[rows, :] = l
 
-        @pl.when(i + 2 < 8)
+        @pl.when(i + 2 < 16)
         def _():
             load(i + 2, slot).start()
 
@@ -314,12 +314,12 @@
             total = part[o, cols] + zr[0, t, cols] + (zr[1, t, cols] + zr[2, t, cols])
             dx = coords_t[o, 0:1] - hx
             dy = coords_t[o, 1:2] - hy
-            scaled = root_three * jnp.sqrt(dx * dx + dy * dy) / lengthscale[0]
-            val = variance[0] * (1.0 + scaled) * jnp.exp(-scaled)
+            scaled = root_three * jnp.sqrt(dx * dx + dy * dy) / lengthscale[...]
+            val = variance[...] * (1.0 + scaled) * jnp.exp(-scaled)
             if nugget:
                 ri = lax.broadcasted_iota(jnp.int32, (32, wide), 0) + first
                 ci = lax.broadcasted_iota(jnp.int32, (32, wide), 1) + job[0][0]
-                val = val + jnp.where(ri == ci, nugget_ref[0], 0.0)
+                val = val + jnp.where(ri == ci, nugget_ref[...], 0.0)
             full[o, cols] = val - total
             return 0
         lax.fori_loop(0, s // 32, body, 0)
@@ -359,6 +359,10 @@
                 across(job, half).wait_send()
                 beside(job, half).wait_send()
 
+    def u_copy(i):
+        cols = pl.ds(0, 768) if i == 0 else pl.ds(768, 256)
+        return pltpu.make_async_copy(full.at[:, cols], u_out.at[:, cols], o_sem.at[i])
+
     load(0, 0).start()
     load(1, 1).start()
     coords_t[...] = jnp.concatenate([coords[...]] * 4, axis=0).T
@@ -380,7 +384,7 @@
         def tk(i, _):
             take(i)
             return 0
-        lax.fori_loop(0, 8, tk, 0)
+        lax.fori_loop(0, 16, tk, 0)
         gram = [((256 * c, 256), 256 * c, 32 * (4 - c), 0, 0, c) for c in range(4)]
         rest = ((0, 1024), 1024, 64, 512, 128, 4)
 
@@ -493,6 +497,7 @@
         lax.fori_loop(0, 8, step, 0)
 
         step_e(rest)
+        u_copy(0).start()
         for job in gram + [rest]:
             job_done(job)
         for k in range(1, 8):
@@ -506,20 +511,15 @@
             arrive(s)
             take(s)
             return 0
-        lax.fori_loop(0, 8, early, 0)
+        lax.fori_loop(0, 16, early, 0)
         lead = 4 + D * (DEEP - 1)
-
-        def wait_only(s, _):
-            arrive(s)
-            return 0
-        lax.fori_loop(8, lead, wait_only, 0)
 
         def block(m, hops=None):
             def cut(t, _):
                 h, l = split(head[pl.ds(pl.multiple_of(m * 128 + t * 16, 16), 16), :])
                 o = pl.ds(pl.multiple_of(t * 16, 16), 16)
-                hh[o, :] = h
-                hl[o, :] = l
+                hb[o, :] = h
+                hb[pl.ds(pl.multiple_of(128 + t * 16, 16), 16), :] = l
                 return 0
             lax.fori_loop(0, 8, cut, 0)
 
@@ -527,11 +527,13 @@
                 if m < 7:
                     arrive(lead + 4 * m + i)
                 r = pl.ds(pl.multiple_of(i * 384, 384), 384)
-                part[r, m * 128:m * 128 + 128] = nt3(ph[r, :], plo[r, :], hh[...], hl[...])
+                both = nt(ph[r, :], hb[...])
+                low = nt(plo[r, :], hb[0:128, :])
+                part[r, m * 128:m * 128 + 128] = both[:, 0:128] + (both[:, 128:256] + low)
                 if hops is not None:
                     @pl.when(lax.rem(i, 2) == 1)
                     def _():
-                        w_hop(0, 4, hops + lax.div(i, 2))
+                        w_hop(0, 8, hops + lax.div(i, 2))
                 return 0
             lax.fori_loop(0, 4, piece, 0)
 
@@ -541,36 +543,36 @@
             if 0 <= t - 1 < 8:
                 step_b(jobs[t - 1])
             if 0 <= t - 2 < 8:
-                step_c(jobs[t - 2], False, True)
+                step_c(jobs[t - 2], False, t - 2 < 6)
             if 0 <= t - 3 < 8:
-                step_d(jobs[t - 3], True)
-            if 0 <= t - 4 < 8:
+                step_d(jobs[t - 3], t - 3 < 6)
+            if 0 <= t - 4 < 6:
                 step_f(jobs[t - 4])
         for m in range(8):
             block(m, 2 * (m - 5) if m >= 5 else None)
             tick(m)
-        w_hops(0, 4, 6, 8)
+        w_hops(0, 8, 6, 7)
         tick(8)
-        w_hops(4, 4, 0, 3)
+        w_hops(0, 8, 7, 9)
         tick(9)
-        w_hops(4, 4, 3, 5)
+        w_hops(0, 8, 9, 10)
         tick(10)
-        w_hops(4, 4, 5, 7)
-        tick(11)
-        w_hops(4, 4, 7, 8)
-        for c in range(8):
+        for c in range(6):
             step_e(jobs[c], True)
+        u_copy(0).start()
+        w_hops(0, 8, 10, 12)
+        for c in (6, 7):
+            step_e(jobs[c], False)
         for q in range(4):
             for k in range(8):
                 wsib(q, k, 1 - core).wait_recv()
-        for job in jobs:
-            job_done(job, True)
+        for c in range(8):
+            job_done(jobs[c], c < 6)
         whole = wbuf.at[pl.ds(0, 512)]
         remote(whole, whole, ws_send, ws_recv.at[0, 0], sibling).wait_send()
 
-    ucp = pltpu.make_async_copy(full, u_out, o_sem.at[0])
-    wcp = pltpu.make_async_copy(wbuf, w_out, o_sem.at[1])
-    ucp.start()
+    u_copy(1).start()
+    wcp = pltpu.make_async_copy(wbuf, w_out, o_sem.at[2])
     wcp.start()
     for (q, e), has in sends.items():
         @pl.when(has)
@@ -582,33 +584,33 @@
             if q == 0:
                 xcopy(e, 0).wait_send()
                 xcopy(e, 1).wait_send()
-    ucp.wait()
+    u_copy(0).wait()
+    u_copy(1).wait()
     wcp.wait()
 
 
 def gather_and_factor(prior, coords, carried, target, scalars):
     vm = pl.BlockSpec(memory_space=pltpu.VMEM)
-    sm = pl.BlockSpec(memory_space=pltpu.SMEM)
     dma = pltpu.SemaphoreType.DMA
     bf = jnp.bfloat16
     return pl.pallas_call(
         kernel,
         out_shape=(jax.ShapeDtypeStruct((1536, 1024), f32), jax.ShapeDtypeStruct((1032, 1024), f32)),
-        in_specs=[pl.BlockSpec(memory_space=pl.ANY), vm, vm, vm, sm, sm, sm],
+        in_specs=[pl.BlockSpec(memory_space=pl.ANY), vm, vm, vm, vm, vm, vm],
         out_specs=(pl.BlockSpec(memory_space=pl.ANY), pl.BlockSpec(memory_space=pl.ANY)),
         scratch_shapes=[
             pltpu.VMEM((1536, 8), f32),
             pltpu.VMEM((1024, 2048), f32),
             pltpu.VMEM((1536, 2048), bf), pltpu.VMEM((1536, 2048), bf),
-            pltpu.VMEM((128, 2048), bf), pltpu.VMEM((128, 2048), bf),
+            pltpu.VMEM((256, 2048), bf),
             pltpu.VMEM((1536, 1024), f32), pltpu.VMEM((768, 1024), f32), pltpu.VMEM((3, 192, 1024), f32),
             pltpu.VMEM((1536, 1024), f32), pltpu.VMEM((1032, 1024), f32), pltpu.VMEM((2, PIECE, 2048), f32),
             pltpu.VMEM((8, 1024), f32), pltpu.VMEM((8, 8, 1024), f32),
             dma((4, 4)), dma((4, CH)), dma((4, 4)), dma((4, 8)), dma, dma((4, 8)), dma((2, 4)), dma((2,)),
-            dma((8, 15)), dma((8, 15)), dma((7,)), dma((7,)), dma((2,)), dma((2,)),
+            dma((8, 15)), dma((8, 15)), dma((7,)), dma((7,)), dma((2,)), dma((3,)),
         ],
         compiler_params=pltpu.CompilerParams(collective_id=1, has_side_effects=True, vmem_limit_bytes=60 << 20),
-    )(prior, coords, carried[None, :], target[None, :], *scalars)
+    )(prior, coords, carried[None, :], target[None, :], *[v.reshape(1, 1) for v in scalars])
 
 
 def panel_kernel(u, w, out, sol, wh, wl):
@@ -640,7 +642,7 @@
         in_specs=[pl.BlockSpec((m, 1024), lambda i: (i, 0)), pl.BlockSpec((1032, 1024), lambda i: (0, 0))],
         out_specs=(pl.BlockSpec((m, 1024), lambda i: (i, 0)), pl.BlockSpec((1, 1024), lambda i: (0, 0))),
         scratch_shapes=[pltpu.VMEM((1024, 1024), jnp.bfloat16)] * 2,
-        compiler_params=pltpu.CompilerParams(vmem_limit_bytes=48 << 20),
+        compiler_params=pltpu.CompilerParams(vmem_limit_bytes=63 << 20),
     )(update, inverse)
 
 

time: 154 us -> 143 us (0.929)
  Pallas kernels: 148 us -> 140 us
  local copies, waits for them, and re-layouts: 2.19 us -> 0 us
    pallas_call x1, Pallas kernels: 136 us -> 126 us  [gather_and_factor(): pl.pallas_call(kernel, out_shape=(jax.ShapeDtypeStruct((1536, 1024), f32)...]
    unnamed x2 -> x0, local copies, waits for them, and re-layouts: 2.19 us -> none
where the time goes in v4:
time: 143 us; the launch traced here: 142 us
  Pallas kernels  140 us (98%)
  between operations  2.58 us (2%)
    pallas_call x1, Pallas kernels, gather_and_factor(): pl.pallas_call(kernel, out_shape=(jax.ShapeDtypeStruct((1536, 1024), f32)...  126 us
    pallas_call x1, Pallas kernels, panel_product(): pl.pallas_call(panel_kernel, grid=(1536 // m,), out_shape=(jax.ShapeDtype...  13.7 us

profile of v4, /device:TPU:13, one launch (start us, length us, event | category | flops | bytes accessed | tf_op | source)
XLA Modules:
  0.0 142.3 jit_solution(18019032106942982848)
XLA Ops:
  2.6 126.1 %shard_map.86 = (f32[1536,1024]{1,0:T(8,128)}, f32[1032,1024]{1,0:T(8,128)}) custom-call(f32[1536,2048]{1,0:T(8,128)} %prior.1, f32[2,1536]{1,0:T(2,128)} %coords.1, f32[1,2048]{1,0:T(1,128)} %bitcast.9, f32[1,1024]{1,0:T(1,128)} %bitcast.10, f32[1,1]{1,0:T(1,128)} %bitcast.6.variance, f32[1,1]{1,0:T(1,128)} %bitcast.7.lengthscale, f32[1,1]{1,0:T(1,128)} %bitcast.8.nugget_ref), custom_call_target="tpu_custom_call" | custom-call | tf_op jit(solution)/shard_map/pallas_call | solution.py:596
  128.7 13.7 %shard_map.87 = (f32[1536,1024]{1,0:T(8,128)}, f32[1,1024]{1,0:T(1,128)}) custom-call(f32[1536,1024]{1,0:T(8,128)} %get-tuple-element.6.u, f32[1032,1024]{1,0:T(8,128)} %get-tuple-element.7.w), custom_call_target="tpu_custom_call" | custom-call | tf_op jit(solution)/shard_map/pallas_call | solution.py:638

commit v5 on v4

--- a/solution.py
+++ b/solution.py
@@ -413,13 +413,13 @@
         step_c(gram[1], True)
 
         def rbody(i, _):
-            r = pl.ds(pl.multiple_of(1024 + lax.div(i, 4) * 256, 256), 256)
-            cc = pl.ds(pl.multiple_of(lax.rem(i, 4) * 256, 256), 256)
+            r = pl.ds(1024, 512)
+            cc = pl.ds(pl.multiple_of(i * 256, 256), 256)
             part[r, cc] = nt3(ph[r, :], plo[r, :], ph[cc, :], plo[cc, :])
             return 0
-        lax.fori_loop(0, 4, rbody, 0)
+        lax.fori_loop(0, 2, rbody, 0)
         step_d(gram[0])
-        lax.fori_loop(4, 8, rbody, 0)
+        lax.fori_loop(2, 4, rbody, 0)
         step_a(rest)
         step_c(gram[2], True)
         n = 1024
@@ -487,12 +487,19 @@
             def _():
                 rs = sr(r)
                 mt = sr(m.T)
-                act = rows >= ks + B
-                gs = sl(jnp.where(act, mm(sl(head[:, pl.ds(ks, B)]), mt), 0.0))
-                for i in range(1, 8):
-                    zap = act[i * B:(i + 1) * B] & inblk
-                    cur = jnp.where(zap, 0.0, head[i * B:(i + 1) * B, 0:n])
-                    head[i * B:(i + 1) * B, 0:n] = cur - mm(gs[i * B:(i + 1) * B], rs)
+
+                def below(i0, i1):
+                    act = rows[i0 * B:i1 * B] >= ks + B
+                    gs = sl(jnp.where(act, mm(sl(head[i0 * B:i1 * B, pl.ds(ks, B)]), mt), 0.0))
+                    for i in range(i0, i1):
+                        o = slice((i - i0) * B, (i - i0 + 1) * B)
+                        cur = jnp.where(act[o] & inblk, 0.0, head[i * B:(i + 1) * B, 0:n])
+                        head[i * B:(i + 1) * B, 0:n] = cur - mm(gs[o], rs)
+
+                @pl.when(k < 3)
+                def _():
+                    below(1, 4)
+                below(4, 8)
             return 0
         lax.fori_loop(0, 8, step, 0)
 
@@ -555,12 +562,12 @@
         tick(8)
         w_hops(0, 8, 7, 9)
         tick(9)
-        w_hops(0, 8, 9, 10)
+        w_hops(0, 8, 9, 11)
         tick(10)
+        w_hops(0, 8, 11, 12)
         for c in range(6):
             step_e(jobs[c], True)
         u_copy(0).start()
-        w_hops(0, 8, 10, 12)
         for c in (6, 7):
             step_e(jobs[c], False)
         for q in range(4):

time: 143 us -> 143 us (level)
  no operation moved by 1% of the time
where the time goes in v5:
time: 143 us
  Pallas kernels  140 us (98%)
  between operations  2.58 us (2%)
    pallas_call x1, Pallas kernels, gather_and_factor(): pl.pallas_call(kernel, out_shape=(jax.ShapeDtypeStruct((1536, 1024), f32)...  127 us
    pallas_call x1, Pallas kernels, panel_product(): pl.pallas_call(panel_kernel, grid=(1536 // m,), out_shape=(jax.ShapeDtype...  13.7 us

profile of v5, /device:TPU:13, one launch (start us, length us, event | category | flops | bytes accessed | tf_op | source)
XLA Modules:
  0.0 142.8 jit_solution(15185213059311888421)
XLA Ops:
  2.6 126.5 %shard_map.86 = (f32[1536,1024]{1,0:T(8,128)}, f32[1032,1024]{1,0:T(8,128)}) custom-call(f32[1536,2048]{1,0:T(8,128)} %prior.1, f32[2,1536]{1,0:T(2,128)} %coords.1, f32[1,2048]{1,0:T(1,128)} %bitcast.9, f32[1,1024]{1,0:T(1,128)} %bitcast.10, f32[1,1]{1,0:T(1,128)} %bitcast.6.variance, f32[1,1]{1,0:T(1,128)} %bitcast.7.lengthscale, f32[1,1]{1,0:T(1,128)} %bitcast.8.nugget_ref), custom_call_target="tpu_custom_call" | custom-call | tf_op jit(solution)/shard_map/pallas_call | solution.py:603
  129.1 13.7 %shard_map.87 = (f32[1536,1024]{1,0:T(8,128)}, f32[1,1024]{1,0:T(1,128)}) custom-call(f32[1536,1024]{1,0:T(8,128)} %get-tuple-element.6.u, f32[1032,1024]{1,0:T(8,128)} %get-tuple-element.7.w), custom_call_target="tpu_custom_call" | custom-call | tf_op jit(solution)/shard_map/pallas_call | solution.py:645
